TPU v7x, 32 devices: a whole 2x2x4 slice. The times are simulated.
32 devices in a mesh: wide: 8 (over z, x), narrow: 4 (over y, core).
Axes of the slice: x: 2, y: 2, z: 4, core: 2. Of those that a mesh axis runs over, the one named last changes fastest.
Arguments:
- solution: float32 [2, 3, 64, 192, 384], P(None, None, 'wide', 'narrow'), may hold values from -4 to 4
- source_term: float32 [2, 3, 64, 192, 384], P(None, None, 'wide', 'narrow'), may hold values from -6 to 6
- permittivity: bfloat16 [64, 192, 384], P('wide', 'narrow'), may hold values from 1 to 12
- inv_top: bfloat16 [16384, 16384], P('wide', 'narrow'), may hold values from -0.015625 to 0.015625
- inv_mid: bfloat16 [2, 8192, 8192], P(None, 'wide', 'narrow'), may hold values from -0.0234375 to 0.0234375
- inv_low: bfloat16 [4, 8192, 8192], P(None, 'wide', 'narrow'), may hold values from -0.0234375 to 0.0234375
- sep_tile: int32 [512, 1], replicated, may hold values from 0 to 31; in each aligned block of 512 rows (0 to 511, 512 to 1023, ...) at most 32 rows name the same one
- sep_cell: int32 [512, 128], replicated, may hold values from 0 to 442367, as said below
Outputs:
- new_solution: float32 [2, 3, 64, 192, 384], P(None, None, 'wide', 'narrow')
- new_residual: float32 [2, 3, 64, 192, 384], P(None, None, 'wide', 'narrow')
Inputs may be any that keep to these rules, and one draw needn't show every extreme that they name: `sep_tile`: the tile index w * 4 + n of the tile at wide index w and narrow index n that holds the block; every tile holds at least one block and at most 32, and some tile holds exactly 32. `sep_cell`: all entries of the array are distinct.
All inputs are finite; a program needn't handle non-finite values.
Results may differ from a plain program's by a relative error of at most 0.0014.
Values may be sent and summed in bfloat16 or wider, within the bound.
No kernel may reach another device: no remote copies, remote signals or barrier semaphores. Data moves between devices by JAX's collectives and lax.ppermute only.
A program may use at most 192 MiB of HBM per device.

v0:
```python
import functools

import jax
import jax.numpy as jnp
import numpy as np
from jax import lax
from jax.experimental import pallas as pl
from jax.experimental.pallas import tpu as pltpu
from jax.sharding import PartitionSpec as P

OMEGA_SQ = 0.5
MIB = 1 << 20

NEAR = ((0, 0), (1, 0), (-1, 0), (0, 1), (0, -1), (-1, 1), (1, -1))


def iota(shape, dim):
    return lax.broadcasted_iota(jnp.int32, shape, dim)


def ahead(x, axis, edge=0.0):
    n = x.shape[axis]
    return jnp.where(iota(x.shape, axis) == n - 1, edge, pltpu.roll(x, n - 1, axis))


def behind(x, axis, edge):
    return jnp.where(iota(x.shape, axis) == 0, edge, pltpu.roll(x, 1, axis))


def faces_kernel(first_ref, last_ref, low_ref, high_ref, xp_ref, xm_ref, yp_ref, ym_ref, d1_ref, d2_ref):
    ex, ey, ez = last_ref[0, 0, 0], last_ref[0, 1, 0], last_ref[0, 2, 0]
    xp_ref[0, 0] = (ey + (ahead(ex, 0) - ex)).astype(xp_ref.dtype)
    xp_ref[0, 1] = (ez + (ahead(ex, 1) - ex)).astype(xp_ref.dtype)
    xm_ref[0, 0] = first_ref[0, 1, 0].astype(xm_ref.dtype)
    xm_ref[0, 1] = first_ref[0, 2, 0].astype(xm_ref.dtype)
    rows = high_ref.shape[3]
    hx, hy, hz = (high_ref[0, c, :, rows - 1, :] for c in range(3))
    yp_ref[0, 0] = (hx + (ahead(hy, 0) - hy)).astype(yp_ref.dtype)
    yp_ref[0, 1] = (hz + (ahead(hy, 1) - hy)).astype(yp_ref.dtype)
    lx, lz = low_ref[0, 0, :, 0, :], low_ref[0, 2, :, 0, :]
    ym_ref[0, 0] = lx.astype(ym_ref.dtype)
    ym_ref[0, 1] = lz.astype(ym_ref.dtype)
    d1_ref[0] = lx[lx.shape[0] - 1 :].astype(d1_ref.dtype)
    d2_ref[0] = hy[:1].astype(d2_ref.dtype)


def faces(field):
    ns, _, cx, cy, cz = field.shape
    half = jnp.bfloat16
    plane, slab = (1, 3, 1, cy, cz), (1, 3, cx, 8, cz)
    wide, narrow, line = (ns, 2, cy, cz), (ns, 2, cx, cz), (ns, 1, cz)
    return pl.pallas_call(
        faces_kernel,
        grid=(ns,),
        in_specs=[
            pl.BlockSpec(plane, lambda s: (s, 0, 0, 0, 0)),
            pl.BlockSpec(plane, lambda s: (s, 0, cx - 1, 0, 0)),
            pl.BlockSpec(slab, lambda s: (s, 0, 0, 0, 0)),
            pl.BlockSpec(slab, lambda s: (s, 0, 0, cy // 8 - 1, 0)),
        ],
        out_specs=[
            pl.BlockSpec((1, 2, cy, cz), lambda s: (s, 0, 0, 0)),
            pl.BlockSpec((1, 2, cy, cz), lambda s: (s, 0, 0, 0)),
            pl.BlockSpec((1, 2, cx, cz), lambda s: (s, 0, 0, 0)),
            pl.BlockSpec((1, 2, cx, cz), lambda s: (s, 0, 0, 0)),
            pl.BlockSpec((1, 1, cz), lambda s: (s, 0, 0)),
            pl.BlockSpec((1, 1, cz), lambda s: (s, 0, 0)),
        ],
        out_shape=[jax.ShapeDtypeStruct(shape, half) for shape in (wide, wide, narrow, narrow, line, line)],
        name="faces",
    )(field, field, field, field)


def curl_plane(own, beyond, back_z, back_y, y_row_x, y_row_z, y_edge_z, y_edge_x):
    ex, ey, ez = own
    hx = (ahead(ez, 0, y_row_z) - ez) - (ahead(ey, 1) - ey)
    hy = (ahead(ex, 1) - ex) - (beyond[1] - ez)
    hz = (beyond[0] - ey) - (ahead(ex, 0, y_row_x) - ex)
    cx = (hz - behind(hz, 0, y_edge_z)) - (hy - behind(hy, 1, ex))
    cy = (hx - behind(hx, 1, -ey)) - (hz - back_z)
    cz = (hy - back_y) - (hx - behind(hx, 0, y_edge_x))
    return cx, cy, cz, hz, hy


def gather_kernel(
    count_ref, sol_ref, next_ref, src_ref, perm_ref, xm_ref, xp_ref, ym_ref, yp_ref, d1_ref, d2_ref, line_ref, depth_ref,
    res_ref, out_ref, lines, turned, back_z, back_y,
):
    i = pl.program_id(0)
    planes = pl.num_programs(0)
    last = i == planes - 1
    ns, _, _, cy, cz = sol_ref.shape
    scaled = OMEGA_SQ * perm_ref[0].astype(jnp.float32)
    f32 = jnp.float32
    row = iota((cy, cz), 0)
    for s in range(ns):
        own = [sol_ref[s, c, 0] for c in range(3)]

        @pl.when(i == 0)
        def _():
            corner = jnp.where(row == cy - 1, d1_ref[s].astype(f32), 0.0)
            back_z[s] = own[1] - (xm_ref[s, 0].astype(f32) + corner)
            back_y[s] = xm_ref[s, 1].astype(f32) - own[2]

        beyond = [jnp.where(last, xp_ref[s, c].astype(f32), next_ref[s, c + 1, 0]) for c in range(2)]
        y_row_x = yp_ref[s, 0, pl.ds(i, 1), :]
        y_row_z = yp_ref[s, 1, pl.ds(i, 1), :]
        edge = ym_ref[s, 0, pl.ds(i, 1), :] + jnp.where(last, d2_ref[s].astype(f32), 0.0)
        curls = curl_plane(
            own, beyond, back_z[s], back_y[s], y_row_x, y_row_z, edge - own[0], own[2] - ym_ref[s, 1, pl.ds(i, 1), :]
        )
        for c in range(3):
            value = src_ref[s, c, 0] - (curls[c] - scaled * own[c])
            res_ref[s, c, 0] = value
            first = pl.multiple_of(c * planes * cy + i * cy, 16)
            lines[pl.ds(first, cy), s * cz : (s + 1) * cz] = value.astype(jnp.bfloat16)
        back_z[s], back_y[s] = curls[3], curls[4]

    @pl.when(last)
    def _():
        out_ref[...] = jnp.zeros_like(out_ref)
        total = lines.shape[0]
        for a in range(total // 128):
            for b in range(ns * cz // 128):
                turned[b * 128 : (b + 1) * 128, a * 128 : (a + 1) * 128] = lines[
                    a * 128 : (a + 1) * 128, b * 128 : (b + 1) * 128
                ].T

        @pl.loop(0, (count_ref[0] + 1) // 2)
        def _(p):
            hot = (iota((total, 256), 0) == line_ref[pl.ds(p, 1), :]).astype(f32).astype(jnp.bfloat16)
            got = jnp.dot(turned[...], hot, preferred_element_type=f32)
            at = iota((cz, 256), 0) == depth_ref[pl.ds(p, 1), :]
            sums = [
                jnp.sum(jnp.where(at, got[s * cz : (s + 1) * cz], 0.0), axis=0, keepdims=True) for s in range(ns)
            ]
            for h in range(2):
                for s in range(ns):
                    out_ref[p, h : h + 1, s * 128 : (s + 1) * 128] = sums[s][:, h * 128 : (h + 1) * 128]


def residual_and_gather(field, source, permittivity, halos, counts, line, depth):
    ns, _, cx, cy, cz = field.shape
    total = 3 * cx * cy
    pairs = line.shape[0]
    plane = (ns, 3, 1, cy, cz)
    whole = lambda x: pl.BlockSpec(x.shape, lambda i, *_: (0,) * x.ndim)
    halos = [h if n in (0, 1) else h.astype(jnp.float32) for n, h in enumerate(halos)]
    grid_spec = pltpu.PrefetchScalarGridSpec(
        num_scalar_prefetch=1,
        grid=(cx,),
        in_specs=[
            pl.BlockSpec(plane, lambda i, *_: (0, 0, i, 0, 0)),
            pl.BlockSpec(plane, lambda i, *_: (0, 0, jnp.minimum(i + 1, cx - 1), 0, 0)),
            pl.BlockSpec(plane, lambda i, *_: (0, 0, i, 0, 0)),
            pl.BlockSpec((1, cy, cz), lambda i, *_: (i, 0, 0)),
            *[whole(h) for h in halos],
            whole(line),
            whole(depth),
        ],
        out_specs=[
            pl.BlockSpec(plane, lambda i, *_: (0, 0, i, 0, 0)),
            pl.BlockSpec((pairs, 2, ns * 128), lambda i, *_: (0, 0, 0)),
        ],
        scratch_shapes=[
            pltpu.VMEM((total, ns * cz), jnp.bfloat16),
            pltpu.VMEM((ns * cz, total), jnp.bfloat16),
            pltpu.VMEM((ns, cy, cz), jnp.float32),
            pltpu.VMEM((ns, cy, cz), jnp.float32),
        ],
    )
    return pl.pallas_call(
        gather_kernel,
        grid_spec=grid_spec,
        out_shape=[
            jax.ShapeDtypeStruct(field.shape, jnp.float32),
            jax.ShapeDtypeStruct((pairs, 2, ns * 128), jnp.float32),
        ],
        compiler_params=pltpu.CompilerParams(vmem_limit_bytes=40 * MIB),
        name="residual_gather",
    )(counts, field, field, source, permittivity, *halos, line, depth)


def fronts_kernel(steps, x_top, x_mid, x_low, top_ref, mid_ref, low_ref, y_ref):
    g = pl.program_id(0)
    starts = (0, steps[0], steps[0] + steps[1])
    base = 0
    for start, count, x_ref, w_ref in zip(starts, steps, (x_top, x_mid, x_low), (top_ref, mid_ref, low_ref), strict=True):
        rows = w_ref.shape[1]

        @pl.when(jnp.logical_and(g >= start, g < start + count))
        def _(start=start, rows=rows, base=base, x_ref=x_ref, w_ref=w_ref):
            at = pl.multiple_of(base + (g - start) * rows, 128)
            y_ref[:, pl.ds(at, rows)] = lax.dot_general(
                x_ref[0], w_ref[0], (((1,), (1,)), ((), ())), preferred_element_type=jnp.float32
            )

        base += count * rows


def fronts(parts, inverses):
    sources = parts[0].shape[1]
    rows = []
    for inv in inverses:
        step = inv.shape[1]
        while step > 256 and step * inv.shape[2] * 2 > 2 * MIB:
            step //= 2
        rows.append(step)
    per = [inv.shape[1] // step for inv, step in zip(inverses, rows, strict=True)]
    steps = [inv.shape[0] * p for inv, p in zip(inverses, per, strict=True)]
    starts = [0, steps[0], steps[0] + steps[1]]
    height = sum(inv.shape[0] * inv.shape[1] for inv in inverses)

    def local(n, g):
        return jnp.clip(g - starts[n], 0, steps[n] - 1)

    x_specs = [
        pl.BlockSpec((1,) + x.shape[1:], functools.partial(lambda g, n: (local(n, g) // per[n], 0, 0), n=n))
        for n, x in enumerate(parts)
    ]
    w_specs = [
        pl.BlockSpec(
            (1, rows[n], inv.shape[2]),
            functools.partial(lambda g, n: (local(n, g) // per[n], local(n, g) % per[n], 0), n=n),
        )
        for n, inv in enumerate(inverses)
    ]
    entries = sum(inv.size for inv in inverses)
    return pl.pallas_call(
        functools.partial(fronts_kernel, tuple(steps)),
        grid=(sum(steps),),
        in_specs=[*x_specs, *w_specs],
        out_specs=pl.BlockSpec((sources, height), lambda g: (0, 0)),
        out_shape=jax.ShapeDtypeStruct((sources, height), jnp.float32),
        compiler_params=pltpu.CompilerParams(vmem_limit_bytes=40 * MIB),
        cost_estimate=pl.CostEstimate(flops=4 * entries, bytes_accessed=2 * entries, transcendentals=0),
        name="fronts",
    )(*parts, *inverses)


def correct_kernel(
    count_ref, sol_ref, res_ref, perm_ref, line_ref, depth_ref, value_ref,
    out_ref, new_ref, delta, x_halo, y_halo, back_z, back_y,
):
    i = pl.program_id(0)
    planes = pl.num_programs(0)
    last = i == planes - 1
    ns, _, _, cy, cz = sol_ref.shape
    pairs = line_ref.shape[0] // len(NEAR)
    f32 = jnp.float32

    @pl.when(i == 0)
    def _():
        delta[...] = jnp.zeros_like(delta)
        x_halo[...] = jnp.zeros_like(x_halo)
        y_halo[...] = jnp.zeros_like(y_halo)
        place = (
            (delta, 0, delta.shape[0]),
            (x_halo, 0, 2 * cy),
            (x_halo, 2 * cy, 3 * cy),
            *[(y_halo, 0, y_halo.shape[0])] * 4,
        )
        for q, (target, first, height) in enumerate(place):

            @pl.loop(0, (count_ref[q] + 1) // 2)
            def _(p, q=q, target=target, first=first, height=height):
                slot = q * pairs + p
                hot = (iota((height, 256), 0) == line_ref[pl.ds(slot, 1), :]).astype(f32).astype(jnp.bfloat16)
                at = iota((cz, 256), 0) == depth_ref[pl.ds(slot, 1), :]
                pair = [value_ref[pl.ds(2 * slot + h, 1), :] for h in range(2)]
                spread = jnp.concatenate(
                    [
                        jnp.where(
                            at, jnp.concatenate([v[:, s * 128 : (s + 1) * 128] for v in pair], axis=1), 0.0
                        ).astype(jnp.bfloat16)
                        for s in range(ns)
                    ],
                    axis=0,
                )
                target[first : first + height, :] += lax.dot_general(
                    hot, spread, (((1,), (1,)), ((), ())), preferred_element_type=f32
                )

    scaled = OMEGA_SQ * perm_ref[0].astype(f32)
    for s in range(ns):
        lanes = slice(s * cz, (s + 1) * cz)

        def plane(c, at, lanes=lanes):
            return delta[pl.ds(pl.multiple_of(c * planes * cy + at * cy, 8), cy), lanes]

        own = [plane(c, i) for c in range(3)]

        @pl.when(i == 0)
        def _(own=own, lanes=lanes, s=s):
            ex, ey, ez = (x_halo[(2 + c) * cy : (3 + c) * cy, lanes] for c in range(3))
            corner = y_halo[5 * planes : 5 * planes + 1, lanes]
            back_z[s] = own[1] - (ey + (ahead(ex, 0, corner) - ex))
            back_y[s] = (ez + (ahead(ex, 1) - ex)) - own[2]

        after = jnp.minimum(i + 1, planes - 1)
        beyond = [jnp.where(last, x_halo[c * cy : (c + 1) * cy, lanes], plane(c + 1, after)) for c in range(2)]
        y_row_x = y_halo[pl.ds(i, 1), lanes]
        y_row_z = y_halo[pl.ds(planes + i, 1), lanes]
        hx, hy, hz = (y_halo[pl.ds((2 + c) * planes + i, 1), lanes] for c in range(3))
        hy_after = jnp.where(
            last, y_halo[5 * planes + 1 : 5 * planes + 2, lanes], y_halo[pl.ds(3 * planes + after, 1), lanes]
        )
        curls = curl_plane(
            own,
            beyond,
            back_z[s],
            back_y[s],
            y_row_x,
            y_row_z,
            (hx + (hy_after - hy)) - own[0],
            own[2] - (hz + (ahead(hy, 1) - hy)),
        )
        for c in range(3):
            out_ref[s, c, 0] = sol_ref[s, c, 0] + own[c]
            new_ref[s, c, 0] = res_ref[s, c, 0] - (curls[c] - scaled * own[c])
        back_z[s], back_y[s] = curls[3], curls[4]


def correct(field, residual, permittivity, counts, line, depth, values):
    ns, _, cx, cy, cz = field.shape
    plane = pl.BlockSpec((ns, 3, 1, cy, cz), lambda i, *_: (0, 0, i, 0, 0))
    whole = lambda x: pl.BlockSpec(x.shape, lambda i, *_: (0,) * x.ndim)
    y_lines = -(-(5 * cx + 2) // 16) * 16
    grid_spec = pltpu.PrefetchScalarGridSpec(
        num_scalar_prefetch=1,
        grid=(cx,),
        in_specs=[
            plane,
            plane,
            pl.BlockSpec((1, cy, cz), lambda i, *_: (i, 0, 0)),
            whole(line),
            whole(depth),
            whole(values),
        ],
        out_specs=[plane, plane],
        scratch_shapes=[
            pltpu.VMEM((3 * cx * cy, ns * cz), jnp.float32),
            pltpu.VMEM((5 * cy, ns * cz), jnp.float32),
            pltpu.VMEM((y_lines, ns * cz), jnp.float32),
            pltpu.VMEM((ns, cy, cz), jnp.float32),
            pltpu.VMEM((ns, cy, cz), jnp.float32),
        ],
    )
    return pl.pallas_call(
        correct_kernel,
        grid_spec=grid_spec,
        out_shape=[jax.ShapeDtypeStruct(field.shape, jnp.float32)] * 2,
        compiler_params=pltpu.CompilerParams(vmem_limit_bytes=40 * MIB),
        name="correct",
    )(counts, field, residual, permittivity, line, depth, values)


def block_rows_of(inverses, wide_count, block_rows):
    per_device = sum(inv.shape[0] * inv.shape[1] for inv in inverses) // block_rows
    table, base = [], 0
    for inv in inverses:
        per = inv.shape[1] // block_rows
        for f in range(inv.shape[0]):
            b = np.arange(per * wide_count)
            table.append(b // per * per_device + base + f * per + b % per)
        base += inv.shape[0] * per
    return np.concatenate(table).astype(np.int32)


def block_columns_of(inverses, narrow_count, block_rows):
    table, base = [], 0
    for inv in inverses:
        per = inv.shape[2] // block_rows
        for _ in range(inv.shape[0]):
            table.append(base + np.arange(per * narrow_count).reshape(narrow_count, per))
            base += per * narrow_count
    return np.concatenate(table, axis=1).astype(np.int32)


def to_all_wide(block, wide_count):
    spread = jnp.broadcast_to(block[None], (wide_count, *block.shape)).reshape(-1, *block.shape[1:])
    return lax.all_to_all(spread, "wide", 0, 0, tiled=True)


def on_device(solution, source_term, permittivity, inv_top, inv_mid, inv_low, sep_tile, sep_cell):
    wide_count, narrow_count = lax.axis_size("wide"), lax.axis_size("narrow")
    my_wide, my_narrow = lax.axis_index("wide"), lax.axis_index("narrow")
    ns, _, cx, cy, cz = solution.shape
    block_count, block_rows = sep_cell.shape
    capacity = max(2, 2 * block_count // (wide_count * narrow_count))
    inverses = (inv_top[None], inv_mid, inv_low)

    xp, xm, yp, ym, d1, d2 = faces(solution)
    up_wide = [(w, w + 1) for w in range(wide_count - 1)]
    up_narrow = [(n, n + 1) for n in range(narrow_count - 1)]
    diagonal = [
        (w * narrow_count + n, (w + 1) * narrow_count + n - 1)
        for w in range(wide_count - 1)
        for n in range(1, narrow_count)
    ]
    flip = lambda pairs: [(b, a) for a, b in pairs]
    halos = (
        lax.ppermute(xp, "wide", up_wide),
        lax.ppermute(xm, "wide", flip(up_wide)),
        lax.ppermute(yp, "narrow", up_narrow),
        lax.ppermute(ym, "narrow", flip(up_narrow)),
        lax.ppermute(d1, ("wide", "narrow"), diagonal),
        lax.ppermute(d2, ("wide", "narrow"), flip(diagonal)),
    )

    block_tile = sep_tile[:, 0]
    block_ids = jnp.arange(block_count, dtype=jnp.int32)
    slot_rank = jnp.sum(
        jnp.logical_and(
            block_tile[:, None] == block_tile[None, :], block_ids[None, :] < block_ids[:, None]
        ).astype(jnp.int32),
        axis=1,
    )
    offsets = np.array(NEAR, np.int32)
    near_wide, near_narrow = my_wide + offsets[:, 0], my_narrow + offsets[:, 1]
    inside = (near_wide >= 0) & (near_wide < wide_count) & (near_narrow >= 0) & (near_narrow < narrow_count)
    near_tile = jnp.where(inside, near_wide * narrow_count + near_narrow, -1)
    named = block_tile[None, :] == near_tile[:, None]
    counts = jnp.sum(named.astype(jnp.int32), axis=1)
    slots = jnp.arange(capacity, dtype=jnp.int32)
    match = jnp.logical_and(named[:, None, :], slot_rank[None, None, :] == slots[None, :, None])
    near_ids = jnp.sum(jnp.where(match, block_ids[None, None, :], 0), axis=2)
    found = slots[None, :] < counts[:, None]
    cells = jnp.take(sep_cell, near_ids.reshape(-1), axis=0).reshape(len(NEAR), capacity, block_rows)
    depth = cells % cz
    row = cells // cz
    part, at_i, at_j = row // (cx * cy), row // cy % cx, row % cy
    rule = (
        (row, row >= 0),
        ((part - 1) * cy + at_j, (part >= 1) & (at_i == 0)),
        (part * cy + at_j, at_i == cx - 1),
        (part // 2 * cx + at_i, (part != 1) & (at_j == 0)),
        ((2 + part) * cx + at_i, at_j == cy - 1),
        (jnp.full_like(row, 5 * cx), (part == 0) & (at_i == cx - 1) & (at_j == 0)),
        (jnp.full_like(row, 5 * cx + 1), (part == 1) & (at_i == 0) & (at_j == cy - 1)),
    )
    line = jnp.stack(
        [jnp.where(found[q, :, None] & keep[q], at[q], -1) for q, (at, keep) in enumerate(rule)]
    )
    line = line.reshape(-1, 2 * block_rows)
    depth = depth.reshape(-1, 2 * block_rows)
    own_pairs = capacity // 2

    residual, picked = residual_and_gather(
        solution, source_term, permittivity, halos, counts, line[:own_pairs], depth[:own_pairs]
    )
    picked = picked.reshape(capacity, ns * block_rows).astype(jnp.bfloat16)
    row_tiles = lax.all_gather(picked, "narrow", axis=0, tiled=True)
    everyone = to_all_wide(row_tiles, wide_count)

    wanted = jnp.asarray(block_columns_of(inverses, narrow_count, block_rows))[my_narrow]
    columns = jnp.take(everyone, block_tile[wanted] * capacity + slot_rank[wanted], axis=0)
    columns = columns.reshape(-1, ns, block_rows).transpose(1, 0, 2).reshape(ns, -1)
    parts, base = [], 0
    for inv in inverses:
        width = inv.shape[0] * inv.shape[2]
        parts.append(columns[:, base : base + width].reshape(ns, inv.shape[0], -1).transpose(1, 0, 2))
        base += width
    partial = fronts(parts, inverses).astype(jnp.bfloat16)
    rows = partial.shape[1] // block_rows
    shares = lax.all_gather(partial.reshape(ns, rows, block_rows), "narrow", axis=0, tiled=False)
    summed = jnp.sum(shares.astype(jnp.float32), axis=0).astype(jnp.bfloat16)
    summed = summed.transpose(1, 0, 2).reshape(rows, ns * block_rows)
    updates = to_all_wide(summed, wide_count)

    place = jnp.asarray(block_rows_of(inverses, wide_count, block_rows))
    values = jnp.take(updates, place[near_ids.reshape(-1)], axis=0).astype(jnp.float32)
    return tuple(correct(solution, residual, permittivity, counts, line, depth, values))


def solution(mesh):
    return jax.shard_map(
        on_device,
        mesh=mesh,
        in_specs=(
            P(None, None, "wide", "narrow", None),
            P(None, None, "wide", "narrow", None),
            P("wide", "narrow", None),
            P("wide", "narrow"),
            P(None, "wide", "narrow"),
            P(None, "wide", "narrow"),
            P(),
            P(),
        ),
        out_specs=(P(None, None, "wide", "narrow", None), P(None, None, "wide", "narrow", None)),
        check_vma=False,
    )
```

profile of v0, /device:TPU:12, one launch (start us, length us, event | category | flops | bytes accessed | tf_op | source)
XLA Modules:
  0.0 169.4 jit_solution(6309656378779246220)
XLA Ops:
  0.7 2.4 %faces.1 = (bf16[2,2,48,384]{3,2,1,0:T(8,128)(2,1)}, bf16[2,2,48,384]{3,2,1,0:T(8,128)(2,1)}, bf16[2,2,8,384]{3,2,1,0:T(8,128)(2,1)}, bf16[2,2,8,384]{3,2,1,0:T(...) custom-call(f32[2,3,8,48,384]{4,3,2,1,0:T(8,128)} %sol_ref.3, f32[2,3,8,48,384]{4,3,2,1,0:T(8,128)} %sol_ref.3, ...), custom_call_target="tpu_custom_call" | custom-call | tf_op jit(solution)/shard_map/faces/pallas_call | solution.py:52
  3.1 2.9 %collective-permute-start.4 = (bf16[2,1,384]{2,1,0:T(2,128)(2,1)}, bf16[2,1,384]{2,1,0:T(2,128)(2,1)S(1)}, u32[]{:S(2)}, u32[]{:S(2)}) collective-permute-start(bf16[2,1,384]{2,1,0:T(2,128)(2,1)} %get-tuple-element.14), channel_id=1, source_target_pairs={{1,4},{2,5},{3,6},{5,8},{6,9},{7,10},{9,12},{10,13},{11,14},{13,16... | collective-permute-start | bytes 4616 | tf_op jit(solution)/shard_map/ppermute | solution.py:407
  6.0 3.7 %collective-permute-start.5 = (bf16[2,1,384]{2,1,0:T(2,128)(2,1)}, bf16[2,1,384]{2,1,0:T(2,128)(2,1)S(1)}, u32[]{:S(2)}, u32[]{:S(2)}) collective-permute-start(bf16[2,1,384]{2,1,0:T(2,128)(2,1)} %get-tuple-element.15), channel_id=1, source_target_pairs={{4,1},{5,2},{6,3},{8,5},{9,6},{10,7},{12,9},{13,10},{14,11},{16,13... | collective-permute-start | bytes 4616 | tf_op jit(solution)/shard_map/ppermute | solution.py:408
  9.7 1.9 %collective-permute-start.2 = (bf16[2,2,8,384]{3,2,1,0:T(8,128)(2,1)}, bf16[2,2,8,384]{3,2,1,0:T(8,128)(2,1)S(1)}, u32[]{:S(2)}, u32[]{:S(2)}) collective-permute-start(bf16[2,2,8,384]{3,2,1,0:T(8,128)(2,1)} %get-tuple-element.12), channel_id=1, source_target_pairs={{0,1},{1,2},{2,3},{4,5},{5,6},{6,7},{8,9},{9,10},{10,11},{12,13},{... | collective-permute-start | bytes 73736 | tf_op jit(solution)/shard_map/ppermute | solution.py:405
  11.7 3.6 %collective-permute-start.3 = (bf16[2,2,8,384]{3,2,1,0:T(8,128)(2,1)}, bf16[2,2,8,384]{3,2,1,0:T(8,128)(2,1)S(1)}, u32[]{:S(2)}, u32[]{:S(2)}) collective-permute-start(bf16[2,2,8,384]{3,2,1,0:T(8,128)(2,1)} %get-tuple-element.13), channel_id=1, source_target_pairs={{1,0},{2,1},{3,2},{5,4},{6,5},{7,6},{9,8},{10,9},{11,10},{13,12},{... | collective-permute-start | bytes 73736 | tf_op jit(solution)/shard_map/ppermute | solution.py:406
  15.3 2.5 %collective-permute-start = (bf16[2,2,48,384]{3,2,1,0:T(8,128)(2,1)}, bf16[2,2,48,384]{3,2,1,0:T(8,128)(2,1)S(1)}, u32[]{:S(2)}, u32[]{:S(2)}) collective-permute-start(bf16[2,2,48,384]{3,2,1,0:T(8,128)(2,1)} %get-tuple-element.10), channel_id=1, source_target_pairs={{0,4},{4,8},{8,12},{12,16},{16,20},{20,24},{24,28},{1,5},{5,9},{9,... | collective-permute-start | bytes 442376 | tf_op jit(solution)/shard_map/ppermute | solution.py:403
  23.4 1.9 %gather_fusion.1 = s32[224]{0:T(256)S(1)} fusion(s32[512]{0:T(512)S(1)} %copy-done.8, s32[1024]{0:T(1024)S(1)} %get-tuple-element.44), kind=kCustom, calls=%fused_computation.1 | custom fusion | bytes 2688 | tf_op jit(solution)/shard_map/gather | solution.py:472
  25.7 4.2 %collective-permute-start.1 = (bf16[2,2,48,384]{3,2,1,0:T(8,128)(2,1)S(1)}, bf16[2,2,48,384]{3,2,1,0:T(8,128)(2,1)S(1)}, u32[]{:S(2)}, u32[]{:S(2)}) collective-permute-start(bf16[2,2,48,384]{3,2,1,0:T(8,128)(2,1)S(1)} %copy-done.12), channel_id=1, source_target_pairs={{4,0},{8,4},{12,8},{16,12},{20,16},{24,20},{28,24},{5,1},{9,5},{13... | collective-permute-start | bytes 442376 | tf_op jit(solution)/shard_map/ppermute | solution.py:404
  30.0 3.1 %collective-permute-done.1.xp_ref = bf16[2,2,48,384]{3,2,1,0:T(8,128)(2,1)S(1)} collective-permute-done((bf16[2,2,48,384]{3,2,1,0:T(8,128)(2,1)S(1)}, bf16[2,2,48,384]{3,2,1,0:T(8,128)(2,1)S(1)}, u32[]{:S(2)}, u32[]{:S(2)}) %collective-permute-start.1) | collective-permute-done | bytes 147488 | tf_op jit(solution)/shard_map/ppermute | solution.py:404
  33.1 2.0 %copy-done.1 = f32[2,3,8,48,384]{4,3,2,1,0:T(8,128)S(1)} copy-done((f32[2,3,8,48,384]{4,3,2,1,0:T(8,128)S(1)}, f32[2,3,8,48,384]{4,3,2,1,0:T(8,128)}, u32[]{:S(2)}) %copy-start.1) | copy-done | bytes 3538968
  35.1 2.0 %copy-done.4 = f32[2,3,8,48,384]{4,3,2,1,0:T(8,128)S(1)} copy-done((f32[2,3,8,48,384]{4,3,2,1,0:T(8,128)S(1)}, f32[2,3,8,48,384]{4,3,2,1,0:T(8,128)}, u32[]{:S(2)}) %copy-start.4) | copy-done | bytes 3538968
  37.1 17.3 %residual_gather.1 = (f32[2,3,8,48,384]{4,3,2,1,0:T(8,128)S(1)}, f32[16,2,256]{2,1,0:T(2,128)S(1)}) custom-call(s32[7]{0:T(128)S(1)} %convert_reduce_fusion.1.count_ref, f32[2,3,8,48,384]{4,3,2,1,0:T(8,128)S(1)} %copy-done.1, f32[2,3,8,48,384]{4,3,2,1,0:T(8,128)S(1)} %copy-done.1, f32[2,3,8,48,384]{4,3,2,1,0:T(8,128)S(1)} %copy-done.4, ...), custom_call_target="tpu_custom_call" | custom-call | tf_op jit(solution)/shard_map/residual_gather/pallas_call | solution.py:172
  54.5 1.8 %copy-done.5 = f32[2,3,8,48,384]{4,3,2,1,0:T(8,128)} copy-done((f32[2,3,8,48,384]{4,3,2,1,0:T(8,128)}, f32[2,3,8,48,384]{4,3,2,1,0:T(8,128)S(1)}, u32[]{:S(2)}) %copy-start.5) | copy-done | bytes 3538968
  56.3 5.2 %all_gather.6 = bf16[128,256]{1,0:T(8,128)(2,1)S(1)} all-gather(bf16[32,256]{1,0:T(8,128)(2,1)S(1)} %convert_element_type.39), channel_id=1, replica_groups=mesh['wide'=8,'narrow'=4] {'narrow'}, dimensions={0}, use_global_device_ids=true | all-gather | bytes 81920 | tf_op jit(solution)/shard_map/all_gather | solution.py:453
  62.4 4.9 %all-to-all-start = ((bf16[8,128,256]{2,1,0:T(8,128)(2,1)}), bf16[8,128,256]{2,1,0:T(8,128)(2,1)S(1)}, u32[]{:S(2)}, u32[]{:S(2)}) async-start(bf16[8,128,256]{2,1,0:T(8,128)(2,1)} %broadcast_in_dim.101), calls=%async_computation | async-start | bytes 1048576 | tf_op jit(solution)/shard_map/all_to_all | solution.py:382
  67.6 13.4 %all-to-all-done = bf16[8,128,256]{2,1,0:T(8,128)(2,1)S(1)} async-done(((bf16[8,128,256]{2,1,0:T(8,128)(2,1)}), bf16[8,128,256]{2,1,0:T(8,128)(2,1)S(1)}, u32[]{:S(2)}, u32[]{:S(2)}) %all-to-all-start) | async-done | bytes 524320 | tf_op jit(solution)/shard_map/all_to_all | solution.py:382
  82.1 3.4 %copy-done.3 = bf16[2,1024,2048]{2,1,0:T(8,128)(2,1)S(1)} copy-done((bf16[2,1024,2048]{2,1,0:T(8,128)(2,1)S(1)}, bf16[2,1024,2048]{2,1,0:T(8,128)(2,1)}, u32[]{:S(2)}) %copy-start.3) | copy-done | bytes 8388632
  85.5 22.6 %fronts.1 = f32[2,8192]{1,0:T(2,128)S(1)} custom-call(bf16[1,2,4096]{2,1,0:T(2,128)(2,1)S(1)} %get-tuple-element.35.x_top, bf16[2,2,2048]{2,1,0:T(2,128)(2,1)S(1)} %bitcast.68, bf16[4,2,2048]{2,1,0:T(2,128)(2,1)S(1)} %bitcast.67, bf16[1,2048,4096]{2,1,0:T(8,128)(2,1)} %bitcast.73, bf16[2,1024,2048]{2,1,0:T(8,128)(2,1)S(1)} %copy-done.3, ...), custom_call_target="tpu_custom_call" | custom-call | flops 83886080 | bytes 41943040 | tf_op jit(solution)/shard_map/fronts/pallas_call | solution.py:229
  108.1 5.4 %all_gather.7 = bf16[4,2,64,128]{3,2,1,0:T(8,128)(2,1)S(1)} all-gather(bf16[1,2,64,128]{3,2,1,0:T(8,128)(2,1)S(1)} %copy.30), channel_id=1, replica_groups=mesh['wide'=8,'narrow'=4] {'narrow'}, dimensions={0}, use_global_device_ids=true | all-gather | bytes 163840 | tf_op jit(solution)/shard_map/all_gather | solution.py:466
  114.3 4.9 %all-to-all-start.1 = ((bf16[8,64,256]{2,1,0:T(8,128)(2,1)}), bf16[8,64,256]{2,1,0:T(8,128)(2,1)S(1)}, u32[]{:S(2)}, u32[]{:S(2)}) async-start(bf16[8,64,256]{2,1,0:T(8,128)(2,1)} %broadcast_in_dim.105), calls=%async_computation.1 | async-start | bytes 524288 | tf_op jit(solution)/shard_map/all_to_all | solution.py:382
  119.5 8.1 %all-to-all-done.1 = bf16[8,64,256]{2,1,0:T(8,128)(2,1)S(1)} async-done(((bf16[8,64,256]{2,1,0:T(8,128)(2,1)}), bf16[8,64,256]{2,1,0:T(8,128)(2,1)S(1)}, u32[]{:S(2)}, u32[]{:S(2)}) %all-to-all-start.1) | async-done | bytes 262176 | tf_op jit(solution)/shard_map/all_to_all | solution.py:382
  128.9 2.0 %copy-done.2 = f32[2,3,8,48,384]{4,3,2,1,0:T(8,128)S(1)} copy-done((f32[2,3,8,48,384]{4,3,2,1,0:T(8,128)S(1)}, f32[2,3,8,48,384]{4,3,2,1,0:T(8,128)}, u32[]{:S(2)}) %copy-start.2) | copy-done | bytes 3538968
  130.9 2.0 %copy-done.6 = f32[2,3,8,48,384]{4,3,2,1,0:T(8,128)S(1)} copy-done((f32[2,3,8,48,384]{4,3,2,1,0:T(8,128)S(1)}, f32[2,3,8,48,384]{4,3,2,1,0:T(8,128)}, u32[]{:S(2)}) %copy-start.6) | copy-done | bytes 3538968
  132.9 36.5 %correct.1 = (f32[2,3,8,48,384]{4,3,2,1,0:T(8,128)}, f32[2,3,8,48,384]{4,3,2,1,0:T(8,128)}) custom-call(s32[7]{0:T(128)S(1)} %convert_reduce_fusion.1.count_ref, f32[2,3,8,48,384]{4,3,2,1,0:T(8,128)S(1)} %copy-done.2, f32[2,3,8,48,384]{4,3,2,1,0:T(8,128)S(1)} %copy-done.6, bf16[8,48,384]{2,1,0:T(8,128)(2,1)S(1)} %copy-done.7, ...), custom_call_target="tpu_custom_call" | custom-call | tf_op jit(solution)/shard_map/correct/pallas_call | solution.py:349
  (86 shorter events, 10.3 us)
Async XLA Ops:
  0.6 21.3 %copy-start = (s32[512,128]{1,0:T(8,128)S(1)}, s32[512,128]{1,0:T(8,128)}, u32[]{:S(2)}) copy-start(s32[512,128]{1,0:T(8,128)} %param.19) | copy-start | bytes 786436
  0.6 17.4 %copy-start.10 = (s32[7]{0:T(128)S(1)}, s32[7]{0:T(128)}, u32[]{:S(2)}) copy-start(s32[7]{0:T(128)} %constant.145.clone) | copy-start | bytes 88
  0.7 17.4 %copy-start.11 = (s32[7]{0:T(128)S(1)}, s32[7]{0:T(128)}, u32[]{:S(2)}) copy-start(s32[7]{0:T(128)} %constant.144.clone) | copy-start | bytes 88
  0.7 17.1 %copy-start.9 = (s32[512,1]{0,1:T(1,128)S(1)}, s32[512,1]{0,1:T(1,128)}, u32[]{:S(2)}) copy-start(s32[512,1]{0,1:T(1,128)} %param.18) | copy-start | bytes 6148
  3.1 20.3 %copy-start.8 = (s32[512]{0:T(512)S(1)}, s32[512]{0:T(512)}, u32[]{:S(2)}) copy-start(s32[512]{0:T(512)} %constant.147.clone) | copy-start | bytes 6148
  3.1 22.6 %copy-start.12 = (bf16[2,2,48,384]{3,2,1,0:T(8,128)(2,1)S(1)}, bf16[2,2,48,384]{3,2,1,0:T(8,128)(2,1)}, u32[]{:S(2)}) copy-start(bf16[2,2,48,384]{3,2,1,0:T(8,128)(2,1)} %get-tuple-element.11) | copy-start | bytes 442372
  3.1 30.0 %copy-start.7 = (bf16[8,48,384]{2,1,0:T(8,128)(2,1)S(1)}, bf16[8,48,384]{2,1,0:T(8,128)(2,1)}, u32[]{:S(2)}) copy-start(bf16[8,48,384]{2,1,0:T(8,128)(2,1)} %perm_ref.3) | copy-start | bytes 884740
  3.1 22.5 %collective-permute-start.4 = (bf16[2,1,384]{2,1,0:T(2,128)(2,1)}, bf16[2,1,384]{2,1,0:T(2,128)(2,1)S(1)}, u32[]{:S(2)}, u32[]{:S(2)}) collective-permute-start(bf16[2,1,384]{2,1,0:T(2,128)(2,1)} %get-tuple-element.14), channel_id=1, source_target_pairs={{1,4},{2,5},{3,6},{5,8},{6,9},{7,10},{9,12},{10,13},{11,14},{13,16... | collective-permute-start | bytes 4616 | tf_op jit(solution)/shard_map/ppermute | solution.py:407
  6.0 23.9 %collective-permute-start.5 = (bf16[2,1,384]{2,1,0:T(2,128)(2,1)}, bf16[2,1,384]{2,1,0:T(2,128)(2,1)S(1)}, u32[]{:S(2)}, u32[]{:S(2)}) collective-permute-start(bf16[2,1,384]{2,1,0:T(2,128)(2,1)} %get-tuple-element.15), channel_id=1, source_target_pairs={{4,1},{5,2},{6,3},{8,5},{9,6},{10,7},{12,9},{13,10},{14,11},{16,13... | collective-permute-start | bytes 4616 | tf_op jit(solution)/shard_map/ppermute | solution.py:408
  9.7 20.3 %collective-permute-start.2 = (bf16[2,2,8,384]{3,2,1,0:T(8,128)(2,1)}, bf16[2,2,8,384]{3,2,1,0:T(8,128)(2,1)S(1)}, u32[]{:S(2)}, u32[]{:S(2)}) collective-permute-start(bf16[2,2,8,384]{3,2,1,0:T(8,128)(2,1)} %get-tuple-element.12), channel_id=1, source_target_pairs={{0,1},{1,2},{2,3},{4,5},{5,6},{6,7},{8,9},{9,10},{10,11},{12,13},{... | collective-permute-start | bytes 73736 | tf_op jit(solution)/shard_map/ppermute | solution.py:405
  11.7 18.4 %collective-permute-start.3 = (bf16[2,2,8,384]{3,2,1,0:T(8,128)(2,1)}, bf16[2,2,8,384]{3,2,1,0:T(8,128)(2,1)S(1)}, u32[]{:S(2)}, u32[]{:S(2)}) collective-permute-start(bf16[2,2,8,384]{3,2,1,0:T(8,128)(2,1)} %get-tuple-element.13), channel_id=1, source_target_pairs={{1,0},{2,1},{3,2},{5,4},{6,5},{7,6},{9,8},{10,9},{11,10},{13,12},{... | collective-permute-start | bytes 73736 | tf_op jit(solution)/shard_map/ppermute | solution.py:406
  15.3 14.7 %collective-permute-start = (bf16[2,2,48,384]{3,2,1,0:T(8,128)(2,1)}, bf16[2,2,48,384]{3,2,1,0:T(8,128)(2,1)S(1)}, u32[]{:S(2)}, u32[]{:S(2)}) collective-permute-start(bf16[2,2,48,384]{3,2,1,0:T(8,128)(2,1)} %get-tuple-element.10), channel_id=1, source_target_pairs={{0,4},{4,8},{8,12},{12,16},{16,20},{20,24},{24,28},{1,5},{5,9},{9,... | collective-permute-start | bytes 442376 | tf_op jit(solution)/shard_map/ppermute | solution.py:403
  25.7 7.5 %collective-permute-start.1 = (bf16[2,2,48,384]{3,2,1,0:T(8,128)(2,1)S(1)}, bf16[2,2,48,384]{3,2,1,0:T(8,128)(2,1)S(1)}, u32[]{:S(2)}, u32[]{:S(2)}) collective-permute-start(bf16[2,2,48,384]{3,2,1,0:T(8,128)(2,1)S(1)} %copy-done.12), channel_id=1, source_target_pairs={{4,0},{8,4},{12,8},{16,12},{20,16},{24,20},{28,24},{5,1},{9,5},{13... | collective-permute-start | bytes 442376 | tf_op jit(solution)/shard_map/ppermute | solution.py:404
  33.1 2.0 %copy-start.1 = (f32[2,3,8,48,384]{4,3,2,1,0:T(8,128)S(1)}, f32[2,3,8,48,384]{4,3,2,1,0:T(8,128)}, u32[]{:S(2)}) copy-start(f32[2,3,8,48,384]{4,3,2,1,0:T(8,128)} %sol_ref.3) | copy-start | bytes 10616836
  35.1 2.0 %copy-start.4 = (f32[2,3,8,48,384]{4,3,2,1,0:T(8,128)S(1)}, f32[2,3,8,48,384]{4,3,2,1,0:T(8,128)}, u32[]{:S(2)}) copy-start(f32[2,3,8,48,384]{4,3,2,1,0:T(8,128)} %src_ref.1) | copy-start | bytes 10616836
  54.5 1.8 %copy-start.5 = (f32[2,3,8,48,384]{4,3,2,1,0:T(8,128)}, f32[2,3,8,48,384]{4,3,2,1,0:T(8,128)S(1)}, u32[]{:S(2)}) copy-start(f32[2,3,8,48,384]{4,3,2,1,0:T(8,128)S(1)} %get-tuple-element.16.res_ref) | copy-start | bytes 10616836
  62.4 18.6 %all-to-all-start = ((bf16[8,128,256]{2,1,0:T(8,128)(2,1)}), bf16[8,128,256]{2,1,0:T(8,128)(2,1)S(1)}, u32[]{:S(2)}, u32[]{:S(2)}) async-start(bf16[8,128,256]{2,1,0:T(8,128)(2,1)} %broadcast_in_dim.101), calls=%async_computation | async-start | bytes 1048576 | tf_op jit(solution)/shard_map/all_to_all | solution.py:382
  82.1 3.4 %copy-start.3 = (bf16[2,1024,2048]{2,1,0:T(8,128)(2,1)S(1)}, bf16[2,1024,2048]{2,1,0:T(8,128)(2,1)}, u32[]{:S(2)}) copy-start(bf16[2,1024,2048]{2,1,0:T(8,128)(2,1)} %mid_ref.1) | copy-start | bytes 25165828
  114.3 13.4 %all-to-all-start.1 = ((bf16[8,64,256]{2,1,0:T(8,128)(2,1)}), bf16[8,64,256]{2,1,0:T(8,128)(2,1)S(1)}, u32[]{:S(2)}, u32[]{:S(2)}) async-start(bf16[8,64,256]{2,1,0:T(8,128)(2,1)} %broadcast_in_dim.105), calls=%async_computation.1 | async-start | bytes 524288 | tf_op jit(solution)/shard_map/all_to_all | solution.py:382
  128.9 2.0 %copy-start.2 = (f32[2,3,8,48,384]{4,3,2,1,0:T(8,128)S(1)}, f32[2,3,8,48,384]{4,3,2,1,0:T(8,128)}, u32[]{:S(2)}) copy-start(f32[2,3,8,48,384]{4,3,2,1,0:T(8,128)} %sol_ref.3) | copy-start | bytes 10616836
  130.9 2.0 %copy-start.6 = (f32[2,3,8,48,384]{4,3,2,1,0:T(8,128)S(1)}, f32[2,3,8,48,384]{4,3,2,1,0:T(8,128)}, u32[]{:S(2)}) copy-start(f32[2,3,8,48,384]{4,3,2,1,0:T(8,128)} %copy-done.5) | copy-start | bytes 10616836
where the time goes:
time: 168 us; the launch traced here: 169 us
  Pallas kernels  78.8 us (47%)
  starting transfers between devices  28.7 us (17%)
  waiting for transfers between devices  24.7 us (15%)
  local copies, waits for them, and re-layouts  22.3 us (13%)
  blocking collectives  10.7 us (6%)
  other arithmetic  3.08 us (2%)
    pallas_call x1, Pallas kernels, correct(): pl.pallas_call(correct_kernel, grid_spec=grid_spec, out_shape=[jax.ShapeD...  36.5 us
    pallas_call x1, Pallas kernels, fronts(): pl.pallas_call(functools.partial(fronts_kernel, tuple(steps)), grid=(sum(...  22.6 us
    all_to_all x2, waiting for transfers between devices, to_all_wide(): return lax.all_to_all(spread, 'wide', 0, 0, tiled=True)  21.6 us
    pallas_call x1, Pallas kernels, residual_and_gather(): pl.pallas_call(gather_kernel, grid_spec=grid_spec, out_shape=[jax.ShapeDt...  17.3 us
    unnamed x28, local copies, waits for them, and re-layouts  13.3 us
    all_to_all x2, starting transfers between devices, to_all_wide(): return lax.all_to_all(spread, 'wide', 0, 0, tiled=True)  9.83 us
    all_gather x1, blocking collectives, on_device(): lax.all_gather(partial.reshape(ns, rows, block_rows), 'narrow', axis=0, t...  5.43 us
    all_gather x1, blocking collectives, on_device(): row_tiles = lax.all_gather(picked, 'narrow', axis=0, tiled=True)  5.25 us
  transfers between devices with their start and end apart: 8, of which 3 were waited for; matrix products, arithmetic and copies ran while one was open for 5% of the time, Pallas kernels for 0%

commit v1 on v0

--- a/solution.py
+++ b/solution.py
@@ -67,6 +67,7 @@
             pl.BlockSpec((1, 1, cz), lambda s: (s, 0, 0)),
         ],
         out_shape=[jax.ShapeDtypeStruct(shape, half) for shape in (wide, wide, narrow, narrow, line, line)],
+        compiler_params=pltpu.CompilerParams(vmem_limit_bytes=60 * MIB),
         name="faces",
     )(field, field, field, field)
 
@@ -84,12 +85,20 @@
 
 def gather_kernel(
     count_ref, sol_ref, next_ref, src_ref, perm_ref, xm_ref, xp_ref, ym_ref, yp_ref, d1_ref, d2_ref, line_ref, depth_ref,
-    res_ref, out_ref, lines, turned, back_z, back_y,
+    res_ref, out_ref, lines, turned, back_z, back_y, y_rows,
 ):
     i = pl.program_id(0)
     planes = pl.num_programs(0)
     last = i == planes - 1
     ns, _, _, cy, cz = sol_ref.shape
+
+    @pl.when(i == 0)
+    def _():
+        for n, ref in enumerate((yp_ref, ym_ref)):
+            for s in range(ns):
+                for c in range(2):
+                    y_rows[n, s, c] = ref[s, c].astype(jnp.float32)
+
     scaled = OMEGA_SQ * perm_ref[0].astype(jnp.float32)
     f32 = jnp.float32
     row = iota((cy, cz), 0)
@@ -103,11 +112,10 @@
             back_y[s] = xm_ref[s, 1].astype(f32) - own[2]
 
         beyond = [jnp.where(last, xp_ref[s, c].astype(f32), next_ref[s, c + 1, 0]) for c in range(2)]
-        y_row_x = yp_ref[s, 0, pl.ds(i, 1), :]
-        y_row_z = yp_ref[s, 1, pl.ds(i, 1), :]
-        edge = ym_ref[s, 0, pl.ds(i, 1), :] + jnp.where(last, d2_ref[s].astype(f32), 0.0)
+        y_row_x, y_row_z = (y_rows[0, s, c, pl.ds(i, 1), :] for c in range(2))
+        edge = y_rows[1, s, 0, pl.ds(i, 1), :] + jnp.where(last, d2_ref[s].astype(f32), 0.0)
         curls = curl_plane(
-            own, beyond, back_z[s], back_y[s], y_row_x, y_row_z, edge - own[0], own[2] - ym_ref[s, 1, pl.ds(i, 1), :]
+            own, beyond, back_z[s], back_y[s], y_row_x, y_row_z, edge - own[0], own[2] - y_rows[1, s, 1, pl.ds(i, 1), :]
         )
         for c in range(3):
             value = src_ref[s, c, 0] - (curls[c] - scaled * own[c])
@@ -126,26 +134,25 @@
                     a * 128 : (a + 1) * 128, b * 128 : (b + 1) * 128
                 ].T
 
-        @pl.loop(0, (count_ref[0] + 1) // 2)
+        group, width = out_ref.shape[1], line_ref.shape[1]
+
+        @pl.loop(0, pl.cdiv(count_ref[0], group))
         def _(p):
-            hot = (iota((total, 256), 0) == line_ref[pl.ds(p, 1), :]).astype(f32).astype(jnp.bfloat16)
+            hot = (iota((total, width), 0) == line_ref[pl.ds(p, 1), :]).astype(f32).astype(jnp.bfloat16)
             got = jnp.dot(turned[...], hot, preferred_element_type=f32)
-            at = iota((cz, 256), 0) == depth_ref[pl.ds(p, 1), :]
-            sums = [
-                jnp.sum(jnp.where(at, got[s * cz : (s + 1) * cz], 0.0), axis=0, keepdims=True) for s in range(ns)
-            ]
-            for h in range(2):
-                for s in range(ns):
-                    out_ref[p, h : h + 1, s * 128 : (s + 1) * 128] = sums[s][:, h * 128 : (h + 1) * 128]
+            at = iota((cz, width), 0) == depth_ref[pl.ds(p, 1), :]
+            for s in range(ns):
+                sums = jnp.sum(jnp.where(at, got[s * cz : (s + 1) * cz], 0.0), axis=0, keepdims=True)
+                for h in range(group):
+                    out_ref[p, h : h + 1, s * 128 : (s + 1) * 128] = sums[:, h * 128 : (h + 1) * 128]
 
 
 def residual_and_gather(field, source, permittivity, halos, counts, line, depth):
     ns, _, cx, cy, cz = field.shape
     total = 3 * cx * cy
-    pairs = line.shape[0]
+    groups, group = line.shape[0], line.shape[1] // 128
     plane = (ns, 3, 1, cy, cz)
     whole = lambda x: pl.BlockSpec(x.shape, lambda i, *_: (0,) * x.ndim)
-    halos = [h if n in (0, 1) else h.astype(jnp.float32) for n, h in enumerate(halos)]
     grid_spec = pltpu.PrefetchScalarGridSpec(
         num_scalar_prefetch=1,
         grid=(cx,),
@@ -160,13 +167,14 @@
         ],
         out_specs=[
             pl.BlockSpec(plane, lambda i, *_: (0, 0, i, 0, 0)),
-            pl.BlockSpec((pairs, 2, ns * 128), lambda i, *_: (0, 0, 0)),
+            pl.BlockSpec((groups, group, ns * 128), lambda i, *_: (0, 0, 0)),
         ],
         scratch_shapes=[
             pltpu.VMEM((total, ns * cz), jnp.bfloat16),
             pltpu.VMEM((ns * cz, total), jnp.bfloat16),
             pltpu.VMEM((ns, cy, cz), jnp.float32),
             pltpu.VMEM((ns, cy, cz), jnp.float32),
+            pltpu.VMEM((2, ns, 2, cx, cz), jnp.float32),
         ],
     )
     return pl.pallas_call(
@@ -174,112 +182,100 @@
         grid_spec=grid_spec,
         out_shape=[
             jax.ShapeDtypeStruct(field.shape, jnp.float32),
-            jax.ShapeDtypeStruct((pairs, 2, ns * 128), jnp.float32),
-        ],
-        compiler_params=pltpu.CompilerParams(vmem_limit_bytes=40 * MIB),
+            jax.ShapeDtypeStruct((groups, group, ns * 128), jnp.float32),
+        ],
+        compiler_params=pltpu.CompilerParams(vmem_limit_bytes=60 * MIB),
         name="residual_gather",
     )(counts, field, field, source, permittivity, *halos, line, depth)
 
 
-def fronts_kernel(steps, x_top, x_mid, x_low, top_ref, mid_ref, low_ref, y_ref):
-    g = pl.program_id(0)
-    starts = (0, steps[0], steps[0] + steps[1])
-    base = 0
-    for start, count, x_ref, w_ref in zip(starts, steps, (x_top, x_mid, x_low), (top_ref, mid_ref, low_ref), strict=True):
-        rows = w_ref.shape[1]
-
-        @pl.when(jnp.logical_and(g >= start, g < start + count))
-        def _(start=start, rows=rows, base=base, x_ref=x_ref, w_ref=w_ref):
-            at = pl.multiple_of(base + (g - start) * rows, 128)
-            y_ref[:, pl.ds(at, rows)] = lax.dot_general(
-                x_ref[0], w_ref[0], (((1,), (1,)), ((), ())), preferred_element_type=jnp.float32
-            )
-
-        base += count * rows
+def fronts_kernel(x_top, x_mid, x_low, top_ref, mid_ref, low_ref, y_ref, top_buf, mid_buf, low_buf, sem):
+    jobs, base = [], 0
+    for x_ref, w_ref, buf in ((x_top, top_ref, top_buf), (x_mid, mid_ref, mid_buf), (x_low, low_ref, low_buf)):
+        count, height, width = w_ref.shape
+        rows = height
+        while rows > 256 and rows * width * 2 > 4 * MIB:
+            rows //= 2
+        for f in range(count):
+            for r in range(0, height, rows):
+                at = pl.ds(r, rows)
+                copy = pltpu.make_async_copy(w_ref.at[f, at], buf.at[f, at], sem.at[len(jobs)])
+                jobs.append((copy, x_ref, buf, f, at, pl.ds(base + r, rows)))
+            base += height
+    for job in jobs:
+        job[0].start()
+    for copy, x_ref, buf, f, at, out in jobs:
+        copy.wait()
+        y_ref[:, out] = lax.dot_general(
+            x_ref[f], buf[f, at], (((1,), (1,)), ((), ())), preferred_element_type=jnp.float32
+        )
 
 
 def fronts(parts, inverses):
     sources = parts[0].shape[1]
-    rows = []
-    for inv in inverses:
-        step = inv.shape[1]
-        while step > 256 and step * inv.shape[2] * 2 > 2 * MIB:
-            step //= 2
-        rows.append(step)
-    per = [inv.shape[1] // step for inv, step in zip(inverses, rows, strict=True)]
-    steps = [inv.shape[0] * p for inv, p in zip(inverses, per, strict=True)]
-    starts = [0, steps[0], steps[0] + steps[1]]
     height = sum(inv.shape[0] * inv.shape[1] for inv in inverses)
-
-    def local(n, g):
-        return jnp.clip(g - starts[n], 0, steps[n] - 1)
-
-    x_specs = [
-        pl.BlockSpec((1,) + x.shape[1:], functools.partial(lambda g, n: (local(n, g) // per[n], 0, 0), n=n))
-        for n, x in enumerate(parts)
-    ]
-    w_specs = [
-        pl.BlockSpec(
-            (1, rows[n], inv.shape[2]),
-            functools.partial(lambda g, n: (local(n, g) // per[n], local(n, g) % per[n], 0), n=n),
-        )
-        for n, inv in enumerate(inverses)
-    ]
     entries = sum(inv.size for inv in inverses)
+    here, there = pl.BlockSpec(memory_space=pltpu.VMEM), pl.BlockSpec(memory_space=pl.ANY)
     return pl.pallas_call(
-        functools.partial(fronts_kernel, tuple(steps)),
-        grid=(sum(steps),),
-        in_specs=[*x_specs, *w_specs],
-        out_specs=pl.BlockSpec((sources, height), lambda g: (0, 0)),
+        fronts_kernel,
+        in_specs=[here] * 3 + [there] * 3,
+        out_specs=here,
         out_shape=jax.ShapeDtypeStruct((sources, height), jnp.float32),
-        compiler_params=pltpu.CompilerParams(vmem_limit_bytes=40 * MIB),
+        scratch_shapes=[pltpu.VMEM(inv.shape, inv.dtype) for inv in inverses] + [pltpu.SemaphoreType.DMA((64,))],
+        compiler_params=pltpu.CompilerParams(vmem_limit_bytes=60 * MIB),
         cost_estimate=pl.CostEstimate(flops=4 * entries, bytes_accessed=2 * entries, transcendentals=0),
         name="fronts",
     )(*parts, *inverses)
 
 
 def correct_kernel(
-    count_ref, sol_ref, res_ref, perm_ref, line_ref, depth_ref, value_ref,
+    count_ref, sol_ref, res_ref, perm_ref, own_line_ref, own_depth_ref, line_ref, depth_ref, value_ref,
     out_ref, new_ref, delta, x_halo, y_halo, back_z, back_y,
 ):
     i = pl.program_id(0)
     planes = pl.num_programs(0)
     last = i == planes - 1
     ns, _, _, cy, cz = sol_ref.shape
-    pairs = line_ref.shape[0] // len(NEAR)
-    f32 = jnp.float32
+    f32, half = jnp.float32, jnp.bfloat16
+    capacity = value_ref.shape[0] // len(NEAR)
+
+    def values_of(first, count):
+        rows = [value_ref[pl.ds(first + h, 1), :] for h in range(count)]
+        return [jnp.concatenate([v[:, s * 128 : (s + 1) * 128] for v in rows], axis=1) for s in range(ns)]
+
+    def times(a, b):
+        return lax.dot_general(a, b, (((1,), (1,)), ((), ())), preferred_element_type=f32)
 
     @pl.when(i == 0)
     def _():
         delta[...] = jnp.zeros_like(delta)
         x_halo[...] = jnp.zeros_like(x_halo)
         y_halo[...] = jnp.zeros_like(y_halo)
-        place = (
-            (delta, 0, delta.shape[0]),
-            (x_halo, 0, 2 * cy),
-            (x_halo, 2 * cy, 3 * cy),
-            *[(y_halo, 0, y_halo.shape[0])] * 4,
-        )
+        own_width = own_line_ref.shape[1]
+        own_group = own_width // 128
+
+        @pl.loop(0, pl.cdiv(count_ref[0], own_group))
+        def _(p):
+            values = values_of(p * own_group, own_group)
+            hot = (iota((delta.shape[0], own_width), 0) == own_line_ref[pl.ds(p, 1), :]).astype(f32).astype(half)
+            at = iota((cz, own_width), 0) == own_depth_ref[pl.ds(p, 1), :]
+            delta[...] += times(hot, jnp.concatenate([jnp.where(at, v, 0.0).astype(half) for v in values], axis=0))
+
+        width = line_ref.shape[1]
+        group = width // 128
+        y_lines = y_halo.shape[1]
+        place = ((x_halo, 0, 2 * cy), (x_halo, 2 * cy, 3 * cy), *[(y_halo, 0, y_lines)] * 4)
         for q, (target, first, height) in enumerate(place):
 
-            @pl.loop(0, (count_ref[q] + 1) // 2)
+            @pl.loop(0, pl.cdiv(count_ref[q + 1], group))
             def _(p, q=q, target=target, first=first, height=height):
-                slot = q * pairs + p
-                hot = (iota((height, 256), 0) == line_ref[pl.ds(slot, 1), :]).astype(f32).astype(jnp.bfloat16)
-                at = iota((cz, 256), 0) == depth_ref[pl.ds(slot, 1), :]
-                pair = [value_ref[pl.ds(2 * slot + h, 1), :] for h in range(2)]
-                spread = jnp.concatenate(
-                    [
-                        jnp.where(
-                            at, jnp.concatenate([v[:, s * 128 : (s + 1) * 128] for v in pair], axis=1), 0.0
-                        ).astype(jnp.bfloat16)
-                        for s in range(ns)
-                    ],
-                    axis=0,
-                )
-                target[first : first + height, :] += lax.dot_general(
-                    hot, spread, (((1,), (1,)), ((), ())), preferred_element_type=f32
-                )
+                row = q * (capacity // group) + p
+                values = values_of((q + 1) * capacity + p * group, group)
+                at = iota((height, width), 0) == line_ref[pl.ds(row, 1), :]
+                hot = (iota((cz, width), 0) == depth_ref[pl.ds(row, 1), :]).astype(f32).astype(half)
+                got = times(jnp.concatenate([jnp.where(at, v, 0.0).astype(half) for v in values], axis=0), hot)
+                for s in range(ns):
+                    target[s, first : first + height] += got[s * height : (s + 1) * height]
 
     scaled = OMEGA_SQ * perm_ref[0].astype(f32)
     for s in range(ns):
@@ -291,19 +287,19 @@
         own = [plane(c, i) for c in range(3)]
 
         @pl.when(i == 0)
-        def _(own=own, lanes=lanes, s=s):
-            ex, ey, ez = (x_halo[(2 + c) * cy : (3 + c) * cy, lanes] for c in range(3))
-            corner = y_halo[5 * planes : 5 * planes + 1, lanes]
+        def _(own=own, s=s):
+            ex, ey, ez = (x_halo[s, (2 + c) * cy : (3 + c) * cy] for c in range(3))
+            corner = y_halo[s, 5 * planes : 5 * planes + 1]
             back_z[s] = own[1] - (ey + (ahead(ex, 0, corner) - ex))
             back_y[s] = (ez + (ahead(ex, 1) - ex)) - own[2]
 
         after = jnp.minimum(i + 1, planes - 1)
-        beyond = [jnp.where(last, x_halo[c * cy : (c + 1) * cy, lanes], plane(c + 1, after)) for c in range(2)]
-        y_row_x = y_halo[pl.ds(i, 1), lanes]
-        y_row_z = y_halo[pl.ds(planes + i, 1), lanes]
-        hx, hy, hz = (y_halo[pl.ds((2 + c) * planes + i, 1), lanes] for c in range(3))
+        beyond = [jnp.where(last, x_halo[s, c * cy : (c + 1) * cy], plane(c + 1, after)) for c in range(2)]
+        y_row_x = y_halo[s, pl.ds(i, 1), :]
+        y_row_z = y_halo[s, pl.ds(planes + i, 1), :]
+        hx, hy, hz = (y_halo[s, pl.ds((2 + c) * planes + i, 1), :] for c in range(3))
         hy_after = jnp.where(
-            last, y_halo[5 * planes + 1 : 5 * planes + 2, lanes], y_halo[pl.ds(3 * planes + after, 1), lanes]
+            last, y_halo[s, 5 * planes + 1 : 5 * planes + 2], y_halo[s, pl.ds(3 * planes + after, 1), :]
         )
         curls = curl_plane(
             own,
@@ -321,7 +317,7 @@
         back_z[s], back_y[s] = curls[3], curls[4]
 
 
-def correct(field, residual, permittivity, counts, line, depth, values):
+def correct(field, residual, permittivity, counts, own_line, own_depth, line, depth, values):
     ns, _, cx, cy, cz = field.shape
     plane = pl.BlockSpec((ns, 3, 1, cy, cz), lambda i, *_: (0, 0, i, 0, 0))
     whole = lambda x: pl.BlockSpec(x.shape, lambda i, *_: (0,) * x.ndim)
@@ -333,15 +329,13 @@
             plane,
             plane,
             pl.BlockSpec((1, cy, cz), lambda i, *_: (i, 0, 0)),
-            whole(line),
-            whole(depth),
-            whole(values),
+            *[whole(x) for x in (own_line, own_depth, line, depth, values)],
         ],
         out_specs=[plane, plane],
         scratch_shapes=[
             pltpu.VMEM((3 * cx * cy, ns * cz), jnp.float32),
-            pltpu.VMEM((5 * cy, ns * cz), jnp.float32),
-            pltpu.VMEM((y_lines, ns * cz), jnp.float32),
+            pltpu.VMEM((ns, 5 * cy, cz), jnp.float32),
+            pltpu.VMEM((ns, y_lines, cz), jnp.float32),
             pltpu.VMEM((ns, cy, cz), jnp.float32),
             pltpu.VMEM((ns, cy, cz), jnp.float32),
         ],
@@ -350,9 +344,9 @@
         correct_kernel,
         grid_spec=grid_spec,
         out_shape=[jax.ShapeDtypeStruct(field.shape, jnp.float32)] * 2,
-        compiler_params=pltpu.CompilerParams(vmem_limit_bytes=40 * MIB),
+        compiler_params=pltpu.CompilerParams(vmem_limit_bytes=60 * MIB),
         name="correct",
-    )(counts, field, residual, permittivity, line, depth, values)
+    )(counts, field, residual, permittivity, own_line, own_depth, line, depth, values)
 
 
 def block_rows_of(inverses, wide_count, block_rows):
@@ -399,14 +393,12 @@
         for n in range(1, narrow_count)
     ]
     flip = lambda pairs: [(b, a) for a, b in pairs]
-    halos = (
-        lax.ppermute(xp, "wide", up_wide),
-        lax.ppermute(xm, "wide", flip(up_wide)),
-        lax.ppermute(yp, "narrow", up_narrow),
-        lax.ppermute(ym, "narrow", flip(up_narrow)),
-        lax.ppermute(d1, ("wide", "narrow"), diagonal),
-        lax.ppermute(d2, ("wide", "narrow"), flip(diagonal)),
-    )
+    from_xm, from_xp = lax.ppermute(xp, "wide", up_wide), lax.ppermute(xm, "wide", flip(up_wide))
+    from_ym = lax.ppermute(yp, "narrow", up_narrow)
+    from_d1 = lax.ppermute(d1, ("wide", "narrow"), diagonal)
+    from_d2 = lax.ppermute(d2, ("wide", "narrow"), flip(diagonal))
+    ym, from_d1 = lax.optimization_barrier((ym, from_d1))
+    halos = (from_xm, from_xp, from_ym, lax.ppermute(ym, "narrow", flip(up_narrow)), from_d1, from_d2)
 
     block_tile = sep_tile[:, 0]
     block_ids = jnp.arange(block_count, dtype=jnp.int32)
@@ -425,6 +417,9 @@
     slots = jnp.arange(capacity, dtype=jnp.int32)
     match = jnp.logical_and(named[:, None, :], slot_rank[None, None, :] == slots[None, :, None])
     near_ids = jnp.sum(jnp.where(match, block_ids[None, None, :], 0), axis=2)
+    near_rows = jnp.sum(
+        jnp.where(match, block_rows_of(inverses, wide_count, block_rows)[None, None, :], 0), axis=2
+    )
     found = slots[None, :] < counts[:, None]
     cells = jnp.take(sep_cell, near_ids.reshape(-1), axis=0).reshape(len(NEAR), capacity, block_rows)
     depth = cells % cz
@@ -442,19 +437,25 @@
     line = jnp.stack(
         [jnp.where(found[q, :, None] & keep[q], at[q], -1) for q, (at, keep) in enumerate(rule)]
     )
-    line = line.reshape(-1, 2 * block_rows)
-    depth = depth.reshape(-1, 2 * block_rows)
-    own_pairs = capacity // 2
+    arrives = (block_tile % narrow_count * wide_count + block_tile // narrow_count) * capacity + slot_rank
+    table = block_columns_of(inverses, narrow_count, block_rows)
+    held_at = jnp.sum(
+        jnp.where(
+            (table[:, :, None] == block_ids) & (np.arange(narrow_count)[:, None, None] == my_narrow), arrives, 0
+        ),
+        axis=(0, 2),
+    )
+    own_width, width = min(8, capacity) * block_rows, min(4, capacity) * block_rows
+    own_line, own_depth = line[0].reshape(-1, own_width), depth[0].reshape(-1, own_width)
+    line, depth = line[1:].reshape(-1, width), depth[1:].reshape(-1, width)
 
     residual, picked = residual_and_gather(
-        solution, source_term, permittivity, halos, counts, line[:own_pairs], depth[:own_pairs]
+        solution, source_term, permittivity, halos, counts, own_line, own_depth
     )
     picked = picked.reshape(capacity, ns * block_rows).astype(jnp.bfloat16)
-    row_tiles = lax.all_gather(picked, "narrow", axis=0, tiled=True)
-    everyone = to_all_wide(row_tiles, wide_count)
-
-    wanted = jnp.asarray(block_columns_of(inverses, narrow_count, block_rows))[my_narrow]
-    columns = jnp.take(everyone, block_tile[wanted] * capacity + slot_rank[wanted], axis=0)
+    everyone = lax.all_gather(to_all_wide(picked, wide_count), "narrow", axis=0, tiled=True)
+
+    columns = jnp.take(everyone, held_at, axis=0)
     columns = columns.reshape(-1, ns, block_rows).transpose(1, 0, 2).reshape(ns, -1)
     parts, base = [], 0
     for inv in inverses:
@@ -468,9 +469,8 @@
     summed = summed.transpose(1, 0, 2).reshape(rows, ns * block_rows)
     updates = to_all_wide(summed, wide_count)
 
-    place = jnp.asarray(block_rows_of(inverses, wide_count, block_rows))
-    values = jnp.take(updates, place[near_ids.reshape(-1)], axis=0).astype(jnp.float32)
-    return tuple(correct(solution, residual, permittivity, counts, line, depth, values))
+    values = jnp.take(updates, near_rows.reshape(-1), axis=0).astype(jnp.float32)
+    return tuple(correct(solution, residual, permittivity, counts, own_line, own_depth, line, depth, values))
 
 
 def solution(mesh):

time: 168 us -> 137 us (0.82)
  the two profiles are of different devices: /device:TPU:12 before, /device:TPU:6 now
where the time goes in v1:
time: 137 us; the launch traced here: 136 us
  Pallas kernels  65.5 us (48%)
  starting transfers between devices  25.8 us (19%)
  blocking collectives  14.8 us (11%)
  waiting for transfers between devices  14.2 us (10%)
  local copies, waits for them, and re-layouts  9.08 us (7%)
  other arithmetic  5.69 us (4%)
    pallas_call x1, Pallas kernels, correct(): pl.pallas_call(correct_kernel, grid_spec=grid_spec, out_shape=[jax.ShapeD...  27 us
    pallas_call x1, Pallas kernels, residual_and_gather(): pl.pallas_call(gather_kernel, grid_spec=grid_spec, out_shape=[jax.ShapeDt...  19.8 us
    pallas_call x1, Pallas kernels, fronts(): pl.pallas_call(fronts_kernel, in_specs=[here] * 3 + [there] * 3, out_spec...  16.3 us
    all_to_all x2, waiting for transfers between devices, to_all_wide(): return lax.all_to_all(spread, 'wide', 0, 0, tiled=True)  13.1 us
    all_gather x1, blocking collectives, on_device(): lax.all_gather(to_all_wide(picked, wide_count), 'narrow', axis=0, tiled=T...  9.42 us
    all_to_all x2, starting transfers between devices, to_all_wide(): return lax.all_to_all(spread, 'wide', 0, 0, tiled=True)  8.67 us
    all_gather x1, blocking collectives, on_device(): lax.all_gather(partial.reshape(ns, rows, block_rows), 'narrow', axis=0, t...  5.43 us
    ppermute x1, starting transfers between devices, on_device(): lax.ppermute(xp, 'wide', up_wide)  4.35 us
  transfers between devices with their start and end apart: 8, of which 3 were waited for; matrix products, arithmetic and copies ran while one was open for 5% of the time, Pallas kernels for 0%

profile of v1, /device:TPU:6, one launch (start us, length us, event | category | flops | bytes accessed | tf_op | source)
XLA Modules:
  0.0 136.1 jit_solution(4634181382864952684)
XLA Ops:
  0.7 2.4 %faces.1 = (bf16[2,2,48,384]{3,2,1,0:T(8,128)(2,1)}, bf16[2,2,48,384]{3,2,1,0:T(8,128)(2,1)}, bf16[2,2,8,384]{3,2,1,0:T(8,128)(2,1)}, bf16[2,2,8,384]{3,2,1,0:T(...) custom-call(f32[2,3,8,48,384]{4,3,2,1,0:T(8,128)} %sol_ref.3, f32[2,3,8,48,384]{4,3,2,1,0:T(8,128)} %sol_ref.3, ...), custom_call_target="tpu_custom_call" | custom-call | tf_op jit(solution)/shard_map/faces/pallas_call | solution.py:52
  3.1 2.8 %collective-permute-start.3 = (bf16[2,1,384]{2,1,0:T(2,128)(2,1)}, bf16[2,1,384]{2,1,0:T(2,128)(2,1)S(1)}, u32[]{:S(2)}, u32[]{:S(2)}) collective-permute-start(bf16[2,1,384]{2,1,0:T(2,128)(2,1)} %get-tuple-element.16), channel_id=1, source_target_pairs={{1,4},{2,5},{3,6},{5,8},{6,9},{7,10},{9,12},{10,13},{11,14},{13,16... | collective-permute-start | bytes 4616 | tf_op jit(solution)/shard_map/ppermute | solution.py:398
  6.0 2.7 %collective-permute-start.5 = (bf16[2,1,384]{2,1,0:T(2,128)(2,1)}, bf16[2,1,384]{2,1,0:T(2,128)(2,1)S(1)}, u32[]{:S(2)}, u32[]{:S(2)}) collective-permute-start(bf16[2,1,384]{2,1,0:T(2,128)(2,1)} %get-tuple-element.19), channel_id=1, source_target_pairs={{4,1},{5,2},{6,3},{8,5},{9,6},{10,7},{12,9},{13,10},{14,11},{16,13... | collective-permute-start | bytes 4616 | tf_op jit(solution)/shard_map/ppermute | solution.py:399
  8.7 1.9 %collective-permute-start.2 = (bf16[2,2,8,384]{3,2,1,0:T(8,128)(2,1)}, bf16[2,2,8,384]{3,2,1,0:T(8,128)(2,1)S(1)}, u32[]{:S(2)}, u32[]{:S(2)}) collective-permute-start(bf16[2,2,8,384]{3,2,1,0:T(8,128)(2,1)} %get-tuple-element.14), channel_id=1, source_target_pairs={{0,1},{1,2},{2,3},{4,5},{5,6},{6,7},{8,9},{9,10},{10,11},{12,13},{... | collective-permute-start | bytes 73736 | tf_op jit(solution)/shard_map/ppermute | solution.py:397
  10.6 4.4 %collective-permute-start = (bf16[2,2,48,384]{3,2,1,0:T(8,128)(2,1)}, bf16[2,2,48,384]{3,2,1,0:T(8,128)(2,1)S(1)}, u32[]{:S(2)}, u32[]{:S(2)}) collective-permute-start(bf16[2,2,48,384]{3,2,1,0:T(8,128)(2,1)} %get-tuple-element.12), channel_id=1, source_target_pairs={{0,4},{4,8},{8,12},{12,16},{16,20},{20,24},{24,28},{1,5},{5,9},{9,... | collective-permute-start | bytes 442376 | tf_op jit(solution)/shard_map/ppermute | solution.py:396
  15.0 1.9 %collective-permute-start.1 = (bf16[2,2,48,384]{3,2,1,0:T(8,128)(2,1)}, bf16[2,2,48,384]{3,2,1,0:T(8,128)(2,1)S(1)}, u32[]{:S(2)}, u32[]{:S(2)}) collective-permute-start(bf16[2,2,48,384]{3,2,1,0:T(8,128)(2,1)} %get-tuple-element.13), channel_id=1, source_target_pairs={{4,0},{8,4},{12,8},{16,12},{20,16},{24,20},{28,24},{5,1},{9,5},{13... | collective-permute-start | bytes 442376 | tf_op jit(solution)/shard_map/ppermute | solution.py:396
  18.0 0.7 gather_fusion
  21.3 3.4 %collective-permute-start.4 = (bf16[2,2,8,384]{3,2,1,0:T(8,128)(2,1)}, bf16[2,2,8,384]{3,2,1,0:T(8,128)(2,1)S(1)}, u32[]{:S(2)}, u32[]{:S(2)}) collective-permute-start(bf16[2,2,8,384]{3,2,1,0:T(8,128)(2,1)} %get-tuple-element.17), channel_id=1, source_target_pairs={{1,0},{2,1},{3,2},{5,4},{6,5},{7,6},{9,8},{10,9},{11,10},{13,12},{... | collective-permute-start | bytes 73736 | tf_op jit(solution)/shard_map/ppermute | solution.py:401
  25.3 1.1 collective-permute-done.4.yp_ref
  27.7 19.8 %residual_gather.1 = (f32[2,3,8,48,384]{4,3,2,1,0:T(8,128)}, f32[4,8,256]{2,1,0:T(8,128)}) custom-call(s32[7]{0:T(128)} %copy-done.6, f32[2,3,8,48,384]{4,3,2,1,0:T(8,128)} %sol_ref.3, f32[2,3,8,48,384]{4,3,2,1,0:T(8,128)} %sol_ref.3, f32[2,3,8,48,384]{4,3,2,1,0:T(8,128)} %src_ref.1, bf16[8,48,384]{2,1,0:T(8,128)(2,1)} %perm_ref.3, ...), custom_call_target="tpu_custom_call" | custom-call | tf_op jit(solution)/shard_map/residual_gather/pallas_call | solution.py:180
  47.5 0.8 convert_bitcast_fusion.1
  48.9 3.3 %all-to-all-start = ((bf16[8,32,256]{2,1,0:T(8,128)(2,1)}), bf16[8,32,256]{2,1,0:T(8,128)(2,1)S(1)}, u32[]{:S(2)}, u32[]{:S(2)}) async-start(bf16[8,32,256]{2,1,0:T(8,128)(2,1)} %broadcast_in_dim.117), calls=%async_computation | async-start | bytes 262144 | tf_op jit(solution)/shard_map/all_to_all | solution.py:376
  53.8 4.0 %all-to-all-done = bf16[8,32,256]{2,1,0:T(8,128)(2,1)S(1)} async-done(((bf16[8,32,256]{2,1,0:T(8,128)(2,1)}), bf16[8,32,256]{2,1,0:T(8,128)(2,1)S(1)}, u32[]{:S(2)}, u32[]{:S(2)}) %all-to-all-start) | async-done | bytes 131104 | tf_op jit(solution)/shard_map/all_to_all | solution.py:376
  57.8 9.4 %all_gather.6 = bf16[1024,256]{1,0:T(8,128)(2,1)S(1)} all-gather(bf16[256,256]{1,0:T(8,128)(2,1)S(1)} %bitcast.70), channel_id=1, replica_groups=mesh['wide'=8,'narrow'=4] {'narrow'}, dimensions={0}, use_global_device_ids=true | all-gather | bytes 655360 | tf_op jit(solution)/shard_map/all_gather | solution.py:456
  67.2 0.8 gather_fusion.1
  69.5 16.3 %fronts.1 = f32[2,8192]{1,0:T(2,128)} custom-call(bf16[1,2,4096]{2,1,0:T(2,128)(2,1)} %get-tuple-element.37.x_top, bf16[2,2,2048]{2,1,0:T(2,128)(2,1)} %bitcast.74, bf16[4,2,2048]{2,1,0:T(2,128)(2,1)} %bitcast.73, bf16[1,2048,4096]{2,1,0:T(8,128)(2,1)} %bitcast.66, bf16[2,1024,2048]{2,1,0:T(8,128)(2,1)} %mid_ref.1, bf16[4,1024,2048]{2,1,0:T(8,128)(2,1)} %low_ref.3), custom_call_target="tpu_custom_call" | custom-call | flops 83886080 | bytes 41943040 | tf_op jit(solution)/shard_map/fronts/pallas_call | solution.py:219
  85.8 0.9 convert_bitcast_fusion
  86.6 5.4 %all_gather.7 = bf16[4,2,64,128]{3,2,1,0:T(8,128)(2,1)S(1)} all-gather(bf16[1,2,64,128]{3,2,1,0:T(8,128)(2,1)S(1)} %copy.32), channel_id=1, replica_groups=mesh['wide'=8,'narrow'=4] {'narrow'}, dimensions={0}, use_global_device_ids=true | all-gather | bytes 163840 | tf_op jit(solution)/shard_map/all_gather | solution.py:467
  92.1 0.7 broadcast_in_dim.121
  92.8 5.3 %all-to-all-start.1 = ((bf16[8,64,256]{2,1,0:T(8,128)(2,1)}), bf16[8,64,256]{2,1,0:T(8,128)(2,1)S(1)}, u32[]{:S(2)}, u32[]{:S(2)}) async-start(bf16[8,64,256]{2,1,0:T(8,128)(2,1)} %broadcast_in_dim.121), calls=%async_computation.1 | async-start | bytes 524288 | tf_op jit(solution)/shard_map/all_to_all | solution.py:376
  98.2 9.1 %all-to-all-done.1 = bf16[8,64,256]{2,1,0:T(8,128)(2,1)S(1)} async-done(((bf16[8,64,256]{2,1,0:T(8,128)(2,1)}), bf16[8,64,256]{2,1,0:T(8,128)(2,1)S(1)}, u32[]{:S(2)}, u32[]{:S(2)}) %all-to-all-start.1) | async-done | bytes 262176 | tf_op jit(solution)/shard_map/all_to_all | solution.py:376
  107.3 1.1 gather_fusion.2
  108.4 0.8 select_convert_fusion.value_ref
  109.2 27.0 %correct.1 = (f32[2,3,8,48,384]{4,3,2,1,0:T(8,128)}, f32[2,3,8,48,384]{4,3,2,1,0:T(8,128)}) custom-call(s32[7]{0:T(128)} %copy-done.6, f32[2,3,8,48,384]{4,3,2,1,0:T(8,128)} %sol_ref.3, f32[2,3,8,48,384]{4,3,2,1,0:T(8,128)} %get-tuple-element.20.res_ref, bf16[8,48,384]{2,1,0:T(8,128)(2,1)} %perm_ref.3, s32[4,1024]{1,0:T(4,128)} %fusion.29.line_ref.own_line_ref, ...), custom_call_target="tpu_custom_call" | custom-call | tf_op jit(solution)/shard_map/correct/pallas_call | solution.py:343
  (88 shorter events, 9.0 us)
Async XLA Ops:
  0.6 17.4 %copy-start = (s32[512,128]{1,0:T(8,128)S(1)}, s32[512,128]{1,0:T(8,128)}, u32[]{:S(2)}) copy-start(s32[512,128]{1,0:T(8,128)} %param.20) | copy-start | bytes 786436
  0.6 16.5 %copy-start.11 = (s32[7]{0:T(128)S(1)}, s32[7]{0:T(128)}, u32[]{:S(2)}) copy-start(s32[7]{0:T(128)} %constant.166.clone) | copy-start | bytes 88
  0.7 16.5 %copy-start.12 = (s32[7]{0:T(128)S(1)}, s32[7]{0:T(128)}, u32[]{:S(2)}) copy-start(s32[7]{0:T(128)} %constant.165.clone) | copy-start | bytes 88
  0.7 16.9 %copy-start.10 = (s32[512]{0:T(512)S(1)}, s32[512]{0:T(512)}, u32[]{:S(2)}) copy-start(s32[512]{0:T(512)} %constant.170) | copy-start | bytes 6148
  0.7 18.8 %copy-start.13 = (s32[4,1,1]{0,2,1:T(1,128)S(1)}, s32[4,1,1]{0,2,1:T(1,128)}, u32[]{:S(2)}) copy-start(s32[4,1,1]{0,2,1:T(1,128)} %constant.169.clone) | copy-start | bytes 52
  0.7 20.2 %copy-start.9 = (s32[4,128]{1,0:T(4,128)S(1)}, s32[4,128]{1,0:T(4,128)}, u32[]{:S(2)}) copy-start(s32[4,128]{1,0:T(4,128)} %constant.171) | copy-start | bytes 6148
  0.7 16.2 %copy-start.3 = (s32[512,1]{0,1:T(1,128)S(1)}, s32[512,1]{0,1:T(1,128)}, u32[]{:S(2)}) copy-start(s32[512,1]{0,1:T(1,128)} %param.19) | copy-start | bytes 6148
  3.1 18.1 %collective-permute-start.3 = (bf16[2,1,384]{2,1,0:T(2,128)(2,1)}, bf16[2,1,384]{2,1,0:T(2,128)(2,1)S(1)}, u32[]{:S(2)}, u32[]{:S(2)}) collective-permute-start(bf16[2,1,384]{2,1,0:T(2,128)(2,1)} %get-tuple-element.16), channel_id=1, source_target_pairs={{1,4},{2,5},{3,6},{5,8},{6,9},{7,10},{9,12},{10,13},{11,14},{13,16... | collective-permute-start | bytes 4616 | tf_op jit(solution)/shard_map/ppermute | solution.py:398
  6.0 19.3 %collective-permute-start.5 = (bf16[2,1,384]{2,1,0:T(2,128)(2,1)}, bf16[2,1,384]{2,1,0:T(2,128)(2,1)S(1)}, u32[]{:S(2)}, u32[]{:S(2)}) collective-permute-start(bf16[2,1,384]{2,1,0:T(2,128)(2,1)} %get-tuple-element.19), channel_id=1, source_target_pairs={{4,1},{5,2},{6,3},{8,5},{9,6},{10,7},{12,9},{13,10},{14,11},{16,13... | collective-permute-start | bytes 4616 | tf_op jit(solution)/shard_map/ppermute | solution.py:399
  8.7 16.6 %collective-permute-start.2 = (bf16[2,2,8,384]{3,2,1,0:T(8,128)(2,1)}, bf16[2,2,8,384]{3,2,1,0:T(8,128)(2,1)S(1)}, u32[]{:S(2)}, u32[]{:S(2)}) collective-permute-start(bf16[2,2,8,384]{3,2,1,0:T(8,128)(2,1)} %get-tuple-element.14), channel_id=1, source_target_pairs={{0,1},{1,2},{2,3},{4,5},{5,6},{6,7},{8,9},{9,10},{10,11},{12,13},{... | collective-permute-start | bytes 73736 | tf_op jit(solution)/shard_map/ppermute | solution.py:397
  10.6 15.7 %collective-permute-start = (bf16[2,2,48,384]{3,2,1,0:T(8,128)(2,1)}, bf16[2,2,48,384]{3,2,1,0:T(8,128)(2,1)S(1)}, u32[]{:S(2)}, u32[]{:S(2)}) collective-permute-start(bf16[2,2,48,384]{3,2,1,0:T(8,128)(2,1)} %get-tuple-element.12), channel_id=1, source_target_pairs={{0,4},{4,8},{8,12},{12,16},{16,20},{20,24},{24,28},{1,5},{5,9},{9,... | collective-permute-start | bytes 442376 | tf_op jit(solution)/shard_map/ppermute | solution.py:396
  15.0 11.4 %collective-permute-start.1 = (bf16[2,2,48,384]{3,2,1,0:T(8,128)(2,1)}, bf16[2,2,48,384]{3,2,1,0:T(8,128)(2,1)S(1)}, u32[]{:S(2)}, u32[]{:S(2)}) collective-permute-start(bf16[2,2,48,384]{3,2,1,0:T(8,128)(2,1)} %get-tuple-element.13), channel_id=1, source_target_pairs={{4,0},{8,4},{12,8},{16,12},{20,16},{24,20},{28,24},{5,1},{9,5},{13... | collective-permute-start | bytes 442376 | tf_op jit(solution)/shard_map/ppermute | solution.py:396
  17.4 8.9 %copy-start.6 = (s32[7]{0:T(128)}, s32[7]{0:T(128)S(1)}, u32[]{:S(2)}) copy-start(s32[7]{0:T(128)S(1)} %convert_reduce_fusion.1.count_ref) | copy-start | bytes 88
  21.3 5.1 %copy-start.7 = (bf16[2,1,384]{2,1,0:T(2,128)(2,1)}, bf16[2,1,384]{2,1,0:T(2,128)(2,1)S(1)}, u32[]{:S(2)}) copy-start(bf16[2,1,384]{2,1,0:T(2,128)(2,1)S(1)} %collective-permute-done.3.d1_ref) | copy-start | bytes 4612
  21.3 5.1 %collective-permute-start.4 = (bf16[2,2,8,384]{3,2,1,0:T(8,128)(2,1)}, bf16[2,2,8,384]{3,2,1,0:T(8,128)(2,1)S(1)}, u32[]{:S(2)}, u32[]{:S(2)}) collective-permute-start(bf16[2,2,8,384]{3,2,1,0:T(8,128)(2,1)} %get-tuple-element.17), channel_id=1, source_target_pairs={{1,0},{2,1},{3,2},{5,4},{6,5},{7,6},{9,8},{10,9},{11,10},{13,12},{... | collective-permute-start | bytes 73736 | tf_op jit(solution)/shard_map/ppermute | solution.py:401
  25.3 1.1 copy-start.8
  25.3 1.1 copy-start.4
  26.3 0.6 copy-start.5
  26.3 0.7 copy-start.1
  27.0 0.7 copy-start.2
  48.9 8.8 %all-to-all-start = ((bf16[8,32,256]{2,1,0:T(8,128)(2,1)}), bf16[8,32,256]{2,1,0:T(8,128)(2,1)S(1)}, u32[]{:S(2)}, u32[]{:S(2)}) async-start(bf16[8,32,256]{2,1,0:T(8,128)(2,1)} %broadcast_in_dim.117), calls=%async_computation | async-start | bytes 262144 | tf_op jit(solution)/shard_map/all_to_all | solution.py:376
  92.8 14.5 %all-to-all-start.1 = ((bf16[8,64,256]{2,1,0:T(8,128)(2,1)}), bf16[8,64,256]{2,1,0:T(8,128)(2,1)S(1)}, u32[]{:S(2)}, u32[]{:S(2)}) async-start(bf16[8,64,256]{2,1,0:T(8,128)(2,1)} %broadcast_in_dim.121), calls=%async_computation.1 | async-start | bytes 524288 | tf_op jit(solution)/shard_map/all_to_all | solution.py:376

commit v2 on v1

v2 whole, which is shorter than its diff:
```python
import jax
import jax.numpy as jnp
import numpy as np
from jax import lax
from jax.experimental import pallas as pl
from jax.experimental.pallas import tpu as pltpu
from jax.sharding import PartitionSpec as P

OMEGA_SQ = 0.5
MIB = 1 << 20

NEAR = ((0, 0), (1, 0), (-1, 0), (0, 1), (0, -1), (-1, 1), (1, -1))


def iota(shape, dim):
    return lax.broadcasted_iota(jnp.int32, shape, dim)


def lane_blocks(x):
    return [x[:, at : at + 128] for at in range(0, x.shape[1], 128)]


def shifted(x, axis, step, edge):
    if axis == 1:
        size, blocks = 128, lane_blocks(x)
        fill = lane_blocks(jnp.broadcast_to(edge, x.shape))
        turned = [pltpu.roll(b, step % size, 1) for b in blocks]
        mask = iota((1, size), 1)
    else:
        size, tiles = 8, x.shape[0] // 8
        turned = pltpu.roll(x.reshape(tiles, size, x.shape[1]), step % size, 1)
        turned = [turned[t] for t in range(tiles)]
        filled = jnp.broadcast_to(edge, (size, x.shape[1])) if jnp.ndim(edge) == 0 or edge.shape[0] == 1 else edge
        fill = [filled[:size]] * tiles
        mask = iota((size, 1), 0)
    if step < 0:
        others = [*turned[1:], fill[-1]]
        mask = mask == size - 1
    else:
        others = [fill[0], *turned[:-1]]
        mask = mask == 0
    return jnp.concatenate([jnp.where(mask, o, t) for o, t in zip(others, turned, strict=True)], axis=axis)


def ahead(x, axis, edge=0.0):
    return shifted(x, axis, -1, edge)


def behind(x, axis, edge):
    return shifted(x, axis, 1, edge)


def rows_kernel(low_ref, high_ref, out_ref):
    top = high_ref.shape[3] - 1
    rows = [low_ref[0, 0, :, 0, :], low_ref[0, 2, :, 0, :], *(high_ref[0, c, :, top, :] for c in range(3))]
    for n, row in enumerate(rows):
        out_ref[0, n] = row.astype(out_ref.dtype)


def outer_rows(field):
    ns, _, cx, cy, cz = field.shape
    slab = (1, 3, cx, 8, cz)
    return pl.pallas_call(
        rows_kernel,
        grid=(ns,),
        in_specs=[
            pl.BlockSpec(slab, lambda s: (s, 0, 0, 0, 0)),
            pl.BlockSpec(slab, lambda s: (s, 0, 0, cy // 8 - 1, 0)),
        ],
        out_specs=pl.BlockSpec((1, 5, cx, cz), lambda s: (s, 0, 0, 0)),
        out_shape=jax.ShapeDtypeStruct((ns, 5, cx, cz), jnp.bfloat16),
        compiler_params=pltpu.CompilerParams(vmem_limit_bytes=60 * MIB),
        name="outer_rows",
    )(field, field)


def near_row(near_ref, side, ref, n, i):
    row = ref[n].astype(jnp.float32)
    return jnp.where(near_ref[2 + side] > 0, row[i : i + 1], 0.0)


def planes_kernel(near_ref, first_ref, last_ref, prev_ref, next_ref, up_ref, down_ref):
    planes = prev_ref.shape[3]
    cy = first_ref.shape[3]
    dtype = up_ref.dtype
    ex, ey, ez = last_ref[0, 0, 0], last_ref[0, 1, 0], last_ref[0, 2, 0]
    past = near_row(near_ref, 1, next_ref.at[0, 0], 0, planes - 1)
    up_ref[0, :cy] = (ey + (ahead(ex, 0, past) - ex)).astype(dtype)
    up_ref[0, cy:] = (ez + (ahead(ex, 1) - ex)).astype(dtype)
    down_ref[0, :cy] = first_ref[0, 1, 0].astype(dtype)
    down_ref[0, cy : 2 * cy] = first_ref[0, 2, 0].astype(dtype)
    before = near_row(near_ref, 0, prev_ref.at[0, 0], 3, 0)
    down_ref[0, 2 * cy :] = jnp.broadcast_to(before, (down_ref.shape[1] - 2 * cy, before.shape[1])).astype(dtype)


def outer_planes(field, near, rows):
    ns, _, cx, cy, cz = field.shape
    plane = (1, 3, 1, cy, cz)
    grid_spec = pltpu.PrefetchScalarGridSpec(
        num_scalar_prefetch=1,
        grid=(ns,),
        in_specs=[
            pl.BlockSpec(plane, lambda s, _: (s, 0, 0, 0, 0)),
            pl.BlockSpec(plane, lambda s, _: (s, 0, cx - 1, 0, 0)),
            pl.BlockSpec((1, 1, 5, cx, cz), lambda s, near: (near[0], s, 0, 0, 0)),
            pl.BlockSpec((1, 1, 5, cx, cz), lambda s, near: (near[1], s, 0, 0, 0)),
        ],
        out_specs=[
            pl.BlockSpec((1, 2 * cy, cz), lambda s, _: (s, 0, 0)),
            pl.BlockSpec((1, 2 * cy + 16, cz), lambda s, _: (s, 0, 0)),
        ],
    )
    return pl.pallas_call(
        planes_kernel,
        grid_spec=grid_spec,
        out_shape=[
            jax.ShapeDtypeStruct((ns, 2 * cy, cz), jnp.bfloat16),
            jax.ShapeDtypeStruct((ns, 2 * cy + 16, cz), jnp.bfloat16),
        ],
        compiler_params=pltpu.CompilerParams(vmem_limit_bytes=60 * MIB),
        name="outer_planes",
    )(near, field, field, rows, rows)


def curl_plane(own, beyond, back_z, back_y, y_row_x, y_row_z, y_edge_z, y_edge_x):
    ex, ey, ez = own
    hx = (ahead(ez, 0, y_row_z) - ez) - (ahead(ey, 1) - ey)
    hy = (ahead(ex, 1) - ex) - (beyond[1] - ez)
    hz = (beyond[0] - ey) - (ahead(ex, 0, y_row_x) - ex)
    cx = (hz - behind(hz, 0, y_edge_z)) - (hy - behind(hy, 1, ex))
    cy = (hx - behind(hx, 1, -ey)) - (hz - back_z)
    cz = (hy - back_y) - (hx - behind(hx, 0, y_edge_x))
    return cx, cy, cz, hz, hy


def magnetic(own, beyond, row_x):
    ex, ey, ez = own
    return (beyond[0] - ey) - (ahead(ex, 0, row_x) - ex), (ahead(ex, 1) - ex) - (beyond[1] - ez)


def spread_rows(near_ref, prev_ref, next_ref, scratch):
    for s in range(scratch.shape[0]):
        for n in range(5):
            side, ref = (1, next_ref) if n < 2 else (0, prev_ref)
            scratch[s, n] = jnp.where(near_ref[2 + side] > 0, ref[0, s, n].astype(jnp.float32), 0.0)


def residual_plane(s, i, own, beyond, back, rows, after, planes, at, scaled, lines):
    cy, cz = own[0].shape
    cx = rows.shape[2]
    row_x, row_z, ex, ey, ez = (rows[s, n, pl.ds(i, 1), :] for n in range(5))
    curls = curl_plane(
        own, beyond, back[0], back[1], row_x, row_z, (ex + (after - ey)) - own[0], own[2] - (ez + (ahead(ey, 1) - ey))
    )
    for c in range(3):
        value = planes[s, c, at] - (curls[c] - scaled * own[c])
        planes[s, c, at] = value
        first = pl.multiple_of((c * cx + i) * cy, 16)
        lines[pl.ds(first, cy), s * cz : (s + 1) * cz] = value.astype(jnp.bfloat16)
    return curls[3], curls[4]


def inner_kernel(
    near_ref, sol_ref, src_ref, perm_ref, prev_ref, over_ref, res_ref, out_ref,
    field, planes, lines, back_z, back_y, rows, field_sem, plane_sem, res_sem, line_sem,
):
    ns, _, cx, cy, _ = field.shape

    def field_copy(i):
        return pltpu.make_async_copy(sol_ref.at[:, :, i], field.at[:, :, i], field_sem.at[i])

    def plane_copy(i):
        return pltpu.make_async_copy(src_ref.at[:, :, i], planes.at[:, :, i], plane_sem.at[i])

    def res_copy(i):
        return pltpu.make_async_copy(planes.at[:, :, i], res_ref.at[:, :, i], res_sem.at[i])

    def line_copy(i, c):
        at = pl.ds(pl.multiple_of((c * cx + i) * cy, 16), cy)
        return pltpu.make_async_copy(lines.at[at], out_ref.at[at], line_sem.at[c, i])

    for i in range(cx):
        field_copy(i).start()
        if 0 < i < cx - 1:
            plane_copy(i).start()
    spread_rows(near_ref, prev_ref, over_ref, rows)
    field_copy(0).wait()
    field_copy(1).wait()
    for s in range(ns):
        first, second = ([field[s, c, i] for c in range(3)] for i in range(2))
        back_z[s], back_y[s] = magnetic(first, second[1:], rows[s, 0, :1])

    @pl.loop(1, cx - 1)
    def _(i):
        field_copy(i + 1).wait()
        plane_copy(i).wait()
        scaled = OMEGA_SQ * perm_ref[i].astype(jnp.float32)
        for s in range(ns):
            own = [field[s, c, i] for c in range(3)]
            beyond = [field[s, c + 1, i + 1] for c in range(2)]
            back_z[s], back_y[s] = residual_plane(
                s, i, own, beyond, (back_z[s], back_y[s]), rows, rows[s, 3, pl.ds(i + 1, 1), :], planes, i, scaled, lines
            )
        res_copy(i).start()
        for c in range(3):
            line_copy(i, c).start()

    @pl.loop(1, cx - 1)
    def _(i):
        res_copy(i).wait()
        for c in range(3):
            line_copy(i, c).wait()


def inner_residual(field, source, permittivity, near, y_rows):
    ns, _, cx, cy, cz = field.shape
    tile_rows = (1, ns, 5, cx, cz)
    anywhere = pl.BlockSpec(memory_space=pl.ANY)
    dma = pltpu.SemaphoreType.DMA
    grid_spec = pltpu.PrefetchScalarGridSpec(
        num_scalar_prefetch=1,
        grid=(1,),
        in_specs=[
            anywhere,
            anywhere,
            pl.BlockSpec((cx, cy, cz), lambda g, _: (0, 0, 0)),
            pl.BlockSpec(tile_rows, lambda g, near: (near[0], 0, 0, 0, 0)),
            pl.BlockSpec(tile_rows, lambda g, near: (near[1], 0, 0, 0, 0)),
        ],
        out_specs=[anywhere, anywhere],
        scratch_shapes=[
            pltpu.VMEM(field.shape, jnp.float32),
            pltpu.VMEM(field.shape, jnp.float32),
            pltpu.VMEM((3 * cx * cy, ns * cz), jnp.bfloat16),
            pltpu.VMEM((ns, cy, cz), jnp.float32),
            pltpu.VMEM((ns, cy, cz), jnp.float32),
            pltpu.VMEM((ns, 5, cx, cz), jnp.float32),
            dma((cx,)),
            dma((cx,)),
            dma((cx,)),
            dma((3, cx)),
        ],
    )
    return pl.pallas_call(
        inner_kernel,
        grid_spec=grid_spec,
        out_shape=[
            jax.ShapeDtypeStruct(field.shape, jnp.float32),
            jax.ShapeDtypeStruct((3 * cx * cy, ns * cz), jnp.bfloat16),
        ],
        compiler_params=pltpu.CompilerParams(vmem_limit_bytes=60 * MIB),
        cost_estimate=pl.CostEstimate(flops=60 * field.size, bytes_accessed=14 * field.size, transcendentals=0),
        name="inner_residual",
    )(near, field, source, permittivity, y_rows, y_rows)


def gather_kernel(
    count_ref, near_ref, sol_ref, src_ref, perm_ref, prev_ref, over_ref, up_ref, down_ref, inner_ref, line_ref, depth_ref, _,
    res_ref, out_ref, field, planes, lines, turned, rows, field_sem, plane_sem, line_sem,
):
    ns, _, cx, cy, cz = sol_ref.shape
    total = lines.shape[0]
    f32 = jnp.float32
    ends = (0, cx - 1)
    field_copies = [
        pltpu.make_async_copy(sol_ref.at[:, :, i], field.at[:, :, n], field_sem.at[n])
        for n, i in enumerate((0, 1, cx - 2, cx - 1))
    ]
    plane_copies = [
        pltpu.make_async_copy(src_ref.at[:, :, i], planes.at[:, :, n], plane_sem.at[n]) for n, i in enumerate(ends)
    ]
    line_copies = []
    for c in range(3):
        at = pl.ds((c * cx + 1) * cy, (cx - 2) * cy)
        line_copies.append(pltpu.make_async_copy(inner_ref.at[at], lines.at[at], line_sem.at[c]))
    res_copies = [
        pltpu.make_async_copy(planes.at[:, :, n], res_ref.at[:, :, i], plane_sem.at[n]) for n, i in enumerate(ends)
    ]
    for copy in field_copies[:2] + plane_copies[:1] + field_copies[2:] + plane_copies[1:] + line_copies:
        copy.start()
    spread_rows(near_ref, prev_ref, over_ref, rows)
    out_ref[...] = jnp.zeros_like(out_ref)

    for copy in field_copies[:2] + plane_copies[:1]:
        copy.wait()
    scaled = OMEGA_SQ * perm_ref[0].astype(f32)
    for s in range(ns):
        own = [field[s, c, 0] for c in range(3)]
        back = own[1] - up_ref[s, :cy].astype(f32), up_ref[s, cy:].astype(f32) - own[2]
        beyond = [field[s, c + 1, 1] for c in range(2)]
        residual_plane(s, 0, own, beyond, back, rows, rows[s, 3, 1:2], planes, 0, scaled, lines)
    res_copies[0].start()

    for copy in field_copies[2:] + plane_copies[1:]:
        copy.wait()
    scaled = OMEGA_SQ * perm_ref[cx - 1].astype(f32)
    for s in range(ns):
        own = [field[s, c, 3] for c in range(3)]
        back = magnetic([field[s, c, 2] for c in range(3)], own[1:], rows[s, 0, cx - 2 : cx - 1])
        beyond = [down_ref[s, c * cy : (c + 1) * cy].astype(f32) for c in range(2)]
        after = down_ref[s, 2 * cy :].astype(f32)[:1]
        residual_plane(s, cx - 1, own, beyond, back, rows, after, planes, 1, scaled, lines)
    res_copies[1].start()

    for copy in line_copies:
        copy.wait()
    for a in range(total // 128):
        for b in range(ns * cz // 128):
            turned[b * 128 : (b + 1) * 128, a * 128 : (a + 1) * 128] = lines[
                a * 128 : (a + 1) * 128, b * 128 : (b + 1) * 128
            ].T
    group, width = out_ref.shape[1], line_ref.shape[1]

    @pl.loop(0, pl.cdiv(count_ref[0], group))
    def _(p):
        hot = (iota((total, width), 0) == line_ref[pl.ds(p, 1), :]).astype(f32).astype(jnp.bfloat16)
        got = jnp.dot(turned[...], hot, preferred_element_type=f32)
        at = iota((cz, width), 0) == depth_ref[pl.ds(p, 1), :]
        for s in range(ns):
            sums = jnp.sum(jnp.where(at, got[s * cz : (s + 1) * cz], 0.0), axis=0, keepdims=True)
            for h in range(group):
                out_ref[p, h : h + 1, s * 128 : (s + 1) * 128] = sums[:, h * 128 : (h + 1) * 128]

    for copy in res_copies:
        copy.wait()


def outer_residual_and_gather(field, source, permittivity, counts, near, y_rows, up, down, residual, inner, line, depth):
    ns, _, cx, cy, cz = field.shape
    total = 3 * cx * cy
    groups, group = line.shape[0], line.shape[1] // 128
    whole = lambda x: pl.BlockSpec(x.shape, lambda g, *_: (0,) * x.ndim)
    tile_rows = (1, ns, 5, cx, cz)
    anywhere = pl.BlockSpec(memory_space=pl.ANY)
    dma = pltpu.SemaphoreType.DMA
    grid_spec = pltpu.PrefetchScalarGridSpec(
        num_scalar_prefetch=2,
        grid=(1,),
        in_specs=[
            anywhere,
            anywhere,
            whole(permittivity),
            pl.BlockSpec(tile_rows, lambda g, _, near: (near[0], 0, 0, 0, 0)),
            pl.BlockSpec(tile_rows, lambda g, _, near: (near[1], 0, 0, 0, 0)),
            whole(up),
            whole(down),
            anywhere,
            whole(line),
            whole(depth),
            anywhere,
        ],
        out_specs=[anywhere, pl.BlockSpec((groups, group, ns * 128), lambda g, *_: (0, 0, 0))],
        scratch_shapes=[
            pltpu.VMEM((ns, 3, 4, cy, cz), jnp.float32),
            pltpu.VMEM((ns, 3, 2, cy, cz), jnp.float32),
            pltpu.VMEM((total, ns * cz), jnp.bfloat16),
            pltpu.VMEM((ns * cz, total), jnp.bfloat16),
            pltpu.VMEM((ns, 5, cx, cz), jnp.float32),
            dma((4,)),
            dma((2,)),
            dma((3,)),
        ],
    )
    return pl.pallas_call(
        gather_kernel,
        grid_spec=grid_spec,
        out_shape=[
            jax.ShapeDtypeStruct(field.shape, jnp.float32),
            jax.ShapeDtypeStruct((groups, group, ns * 128), jnp.float32),
        ],
        input_output_aliases={12: 0},
        compiler_params=pltpu.CompilerParams(vmem_limit_bytes=60 * MIB),
        name="outer_residual_gather",
    )(counts, near, field, source, permittivity, y_rows, y_rows, up, down, inner, line, depth, residual)


def fronts_kernel(x_top, x_mid, x_low, top_ref, mid_ref, low_ref, y_ref, top_buf, mid_buf, low_buf, sem):
    jobs, base = [], 0
    for x_ref, w_ref, buf in ((x_top, top_ref, top_buf), (x_mid, mid_ref, mid_buf), (x_low, low_ref, low_buf)):
        count, height, width = w_ref.shape
        rows = height
        while rows > 256 and rows * width * 2 > 4 * MIB:
            rows //= 2
        for f in range(count):
            for r in range(0, height, rows):
                at = pl.ds(r, rows)
                copy = pltpu.make_async_copy(w_ref.at[f, at], buf.at[f, at], sem.at[len(jobs)])
                jobs.append((copy, x_ref, buf, f, at, pl.ds(base + r, rows)))
            base += height
    for job in jobs:
        job[0].start()
    for copy, x_ref, buf, f, at, out in jobs:
        copy.wait()
        y_ref[:, out] = lax.dot_general(
            x_ref[f], buf[f, at], (((1,), (1,)), ((), ())), preferred_element_type=jnp.float32
        )


def fronts(parts, inverses):
    sources = parts[0].shape[1]
    height = sum(inv.shape[0] * inv.shape[1] for inv in inverses)
    entries = sum(inv.size for inv in inverses)
    here, there = pl.BlockSpec(memory_space=pltpu.VMEM), pl.BlockSpec(memory_space=pl.ANY)
    return pl.pallas_call(
        fronts_kernel,
        in_specs=[here] * 3 + [there] * 3,
        out_specs=here,
        out_shape=jax.ShapeDtypeStruct((sources, height), jnp.float32),
        scratch_shapes=[pltpu.VMEM(inv.shape, inv.dtype) for inv in inverses] + [pltpu.SemaphoreType.DMA((64,))],
        compiler_params=pltpu.CompilerParams(vmem_limit_bytes=60 * MIB),
        cost_estimate=pl.CostEstimate(flops=4 * entries, bytes_accessed=2 * entries, transcendentals=0),
        name="fronts",
    )(*parts, *inverses)


def correct_kernel(
    count_ref, sol_ref, res_ref, perm_ref, own_line_ref, own_depth_ref, line_ref, depth_ref, value_ref,
    out_ref, new_ref, field, residual, delta, x_halo, y_halo, back_z, back_y, in_sem, out_sem,
):
    ns, _, planes, cy, cz = sol_ref.shape
    f32, half = jnp.float32, jnp.bfloat16

    def copies_in(i):
        return [
            pltpu.make_async_copy(ref.at[:, :, i], buf.at[:, :, i], in_sem.at[n, i])
            for n, (ref, buf) in enumerate(((sol_ref, field), (res_ref, residual)))
        ]

    def copies_out(i):
        return [
            pltpu.make_async_copy(buf.at[:, :, i], ref.at[:, :, i], out_sem.at[n, i])
            for n, (ref, buf) in enumerate(((out_ref, field), (new_ref, residual)))
        ]

    for i in range(planes):
        for copy in copies_in(i):
            copy.start()
    capacity = value_ref.shape[0] // len(NEAR)

    def values_of(first, count):
        rows = [value_ref[pl.ds(first + h, 1), :] for h in range(count)]
        return [jnp.concatenate([v[:, s * 128 : (s + 1) * 128] for v in rows], axis=1) for s in range(ns)]

    def times(a, b):
        return lax.dot_general(a, b, (((1,), (1,)), ((), ())), preferred_element_type=f32)

    x_halo[...] = jnp.zeros_like(x_halo)
    y_halo[...] = jnp.zeros_like(y_halo)
    own_width = own_line_ref.shape[1]
    own_group = own_width // 128

    def own_part(p):
        values = values_of(p * own_group, own_group)
        hot = (iota((delta.shape[0], own_width), 0) == own_line_ref[pl.ds(p, 1), :]).astype(f32).astype(half)
        at = iota((cz, own_width), 0) == own_depth_ref[pl.ds(p, 1), :]
        return times(hot, jnp.concatenate([jnp.where(at, v, 0.0).astype(half) for v in values], axis=0))

    delta[...] = own_part(0)

    @pl.loop(1, pl.cdiv(count_ref[0], own_group))
    def _(p):
        delta[...] += own_part(p)

    width = line_ref.shape[1]
    group = width // 128
    place = (
        (x_halo, 0, 2 * cy),
        (x_halo, 2 * cy, 3 * cy),
        (y_halo, 0, 2 * planes),
        (y_halo, 2 * planes, 3 * planes),
        (y_halo, 5 * planes, 8),
        (y_halo, 5 * planes, 8),
    )
    for q, (target, first, height) in enumerate(place):

        @pl.loop(0, pl.cdiv(count_ref[q + 1], group))
        def _(p, q=q, target=target, first=first, height=height):
            row = q * (capacity // group) + p

            @pl.when(count_ref[len(NEAR) + row] > 0)
            def _():
                values = values_of((q + 1) * capacity + p * group, group)
                at = iota((height, width), 0) == line_ref[pl.ds(row, 1), :]
                hot = (iota((cz, width), 0) == depth_ref[pl.ds(row, 1), :]).astype(f32).astype(half)
                got = times(jnp.concatenate([jnp.where(at, v, 0.0) for v in values], axis=0).astype(half), hot)
                for s in range(ns):
                    target[s, first : first + height] += got[s * height : (s + 1) * height]

    def plane(s, c, i):
        return delta[pl.ds(pl.multiple_of((c * planes + i) * cy, 8), cy), s * cz : (s + 1) * cz]

    for s in range(ns):
        ex, ey, ez = (x_halo[s, (2 + c) * cy : (3 + c) * cy] for c in range(3))
        corner = y_halo[s, 5 * planes : 5 * planes + 1]
        back_z[s] = plane(s, 1, 0) - (ey + (ahead(ex, 0, corner) - ex))
        back_y[s] = (ez + (ahead(ex, 1) - ex)) - plane(s, 2, 0)

    @pl.loop(0, planes)
    def _(i):
        last = i == planes - 1
        after = jnp.minimum(i + 1, planes - 1)
        scaled = OMEGA_SQ * perm_ref[i].astype(f32)
        for copy in copies_in(i):
            copy.wait()
        for s in range(ns):
            own = [plane(s, c, i) for c in range(3)]
            beyond = [jnp.where(last, x_halo[s, c * cy : (c + 1) * cy], plane(s, c + 1, after)) for c in range(2)]
            y_row_x = y_halo[s, pl.ds(i, 1), :]
            y_row_z = y_halo[s, pl.ds(planes + i, 1), :]
            hx, hy, hz = (y_halo[s, pl.ds((2 + c) * planes + i, 1), :] for c in range(3))
            hy_after = jnp.where(
                last, y_halo[s, 5 * planes + 1 : 5 * planes + 2], y_halo[s, pl.ds(3 * planes + after, 1), :]
            )
            curls = curl_plane(
                own,
                beyond,
                back_z[s],
                back_y[s],
                y_row_x,
                y_row_z,
                (hx + (hy_after - hy)) - own[0],
                own[2] - (hz + (ahead(hy, 1) - hy)),
            )
            for c in range(3):
                field[s, c, i] += own[c]
                residual[s, c, i] -= curls[c] - scaled * own[c]
            back_z[s], back_y[s] = curls[3], curls[4]
        for copy in copies_out(i):
            copy.start()

    @pl.loop(0, planes)
    def _(i):
        for copy in copies_out(i):
            copy.wait()


def correct(field, residual, permittivity, counts, own_line, own_depth, line, depth, values):
    ns, _, cx, cy, cz = field.shape
    anywhere = pl.BlockSpec(memory_space=pl.ANY)
    whole = lambda x: pl.BlockSpec(x.shape, lambda g, *_: (0,) * x.ndim)
    y_lines = 5 * cx + 8
    grid_spec = pltpu.PrefetchScalarGridSpec(
        num_scalar_prefetch=1,
        grid=(1,),
        in_specs=[
            anywhere,
            anywhere,
            *[whole(x) for x in (permittivity, own_line, own_depth, line, depth, values)],
        ],
        out_specs=[anywhere, anywhere],
        scratch_shapes=[
            pltpu.VMEM(field.shape, jnp.float32),
            pltpu.VMEM(field.shape, jnp.float32),
            pltpu.VMEM((3 * cx * cy, ns * cz), jnp.float32),
            pltpu.VMEM((ns, 5 * cy, cz), jnp.float32),
            pltpu.VMEM((ns, y_lines, cz), jnp.float32),
            pltpu.VMEM((ns, cy, cz), jnp.float32),
            pltpu.VMEM((ns, cy, cz), jnp.float32),
            pltpu.SemaphoreType.DMA((2, cx)),
            pltpu.SemaphoreType.DMA((2, cx)),
        ],
    )
    return pl.pallas_call(
        correct_kernel,
        grid_spec=grid_spec,
        out_shape=[jax.ShapeDtypeStruct(field.shape, jnp.float32)] * 2,
        compiler_params=pltpu.CompilerParams(vmem_limit_bytes=60 * MIB),
        name="correct",
    )(counts, field, residual, permittivity, own_line, own_depth, line, depth, values)


def block_rows_of(inverses, wide_count, block_rows):
    per_device = sum(inv.shape[0] * inv.shape[1] for inv in inverses) // block_rows
    table, base = [], 0
    for inv in inverses:
        per = inv.shape[1] // block_rows
        for f in range(inv.shape[0]):
            b = np.arange(per * wide_count)
            table.append(b // per * per_device + base + f * per + b % per)
        base += inv.shape[0] * per
    return np.concatenate(table).astype(np.int32)


def block_columns_of(inverses, narrow_count, block_rows):
    table, base = [], 0
    for inv in inverses:
        per = inv.shape[2] // block_rows
        for _ in range(inv.shape[0]):
            table.append(base + np.arange(per * narrow_count).reshape(narrow_count, per))
            base += per * narrow_count
    return np.concatenate(table, axis=1).astype(np.int32)


def to_all_wide(block, wide_count):
    spread = jnp.broadcast_to(block[None], (wide_count, *block.shape)).reshape(-1, *block.shape[1:])
    return lax.all_to_all(spread, "wide", 0, 0, tiled=True)


def on_device(solution, source_term, permittivity, inv_top, inv_mid, inv_low, sep_tile, sep_cell):
    wide_count, narrow_count = lax.axis_size("wide"), lax.axis_size("narrow")
    my_wide, my_narrow = lax.axis_index("wide"), lax.axis_index("narrow")
    ns, _, cx, cy, cz = solution.shape
    block_count, block_rows = sep_cell.shape
    capacity = max(2, 2 * block_count // (wide_count * narrow_count))
    inverses = (inv_top[None], inv_mid, inv_low)

    near = jnp.stack(
        [
            jnp.maximum(my_narrow - 1, 0),
            jnp.minimum(my_narrow + 1, narrow_count - 1),
            (my_narrow > 0).astype(jnp.int32),
            (my_narrow < narrow_count - 1).astype(jnp.int32),
        ]
    )
    y_rows = lax.all_gather(outer_rows(solution), "narrow", axis=0, tiled=False)
    to_up, to_down = outer_planes(solution, near, y_rows)
    steps = [(w, w + 1) for w in range(wide_count - 1)]
    up = lax.ppermute(to_up, "wide", steps)
    down = lax.ppermute(to_down, "wide", [(b, a) for a, b in steps])
    inner, inner_lines = inner_residual(solution, source_term, permittivity, near, y_rows)

    block_tile = sep_tile[:, 0]
    block_ids = jnp.arange(block_count, dtype=jnp.int32)
    slot_rank = jnp.sum(
        jnp.logical_and(
            block_tile[:, None] == block_tile[None, :], block_ids[None, :] < block_ids[:, None]
        ).astype(jnp.int32),
        axis=1,
    )
    offsets = np.array(NEAR, np.int32)
    near_wide, near_narrow = my_wide + offsets[:, 0], my_narrow + offsets[:, 1]
    inside = (near_wide >= 0) & (near_wide < wide_count) & (near_narrow >= 0) & (near_narrow < narrow_count)
    near_tile = jnp.where(inside, near_wide * narrow_count + near_narrow, -1)
    named = block_tile[None, :] == near_tile[:, None]
    counts = jnp.sum(named.astype(jnp.int32), axis=1)
    slots = jnp.arange(capacity, dtype=jnp.int32)
    match = jnp.logical_and(named[:, None, :], slot_rank[None, None, :] == slots[None, :, None])
    near_ids = jnp.sum(jnp.where(match, block_ids[None, None, :], 0), axis=2)
    near_rows = jnp.sum(
        jnp.where(match, block_rows_of(inverses, wide_count, block_rows)[None, None, :], 0), axis=2
    )
    found = slots[None, :] < counts[:, None]
    cells = jnp.take(sep_cell, near_ids.reshape(-1), axis=0).reshape(len(NEAR), capacity, block_rows)
    depth = cells % cz
    row = cells // cz
    part, at_i, at_j = row // (cx * cy), row // cy % cx, row % cy
    rule = (
        (row, row >= 0),
        ((part - 1) * cy + at_j, (part >= 1) & (at_i == 0)),
        (part * cy + at_j, at_i == cx - 1),
        (part // 2 * cx + at_i, (part != 1) & (at_j == 0)),
        (part * cx + at_i, at_j == cy - 1),
        (jnp.zeros_like(row), (part == 0) & (at_i == cx - 1) & (at_j == 0)),
        (jnp.ones_like(row), (part == 1) & (at_i == 0) & (at_j == cy - 1)),
    )
    line = jnp.stack(
        [jnp.where(found[q, :, None] & keep[q], at[q], -1) for q, (at, keep) in enumerate(rule)]
    )
    arrives = (block_tile % narrow_count * wide_count + block_tile // narrow_count) * capacity + slot_rank
    table = block_columns_of(inverses, narrow_count, block_rows)
    held_at = jnp.sum(
        jnp.where(
            (table[:, :, None] == block_ids) & (np.arange(narrow_count)[:, None, None] == my_narrow), arrives, 0
        ),
        axis=(0, 2),
    )
    own_width, width = min(8, capacity) * block_rows, min(4, capacity) * block_rows
    own_line, own_depth = line[0].reshape(-1, own_width), depth[0].reshape(-1, own_width)
    line, depth = line[1:].reshape(-1, width), depth[1:].reshape(-1, width)
    loads = jnp.concatenate([counts, jnp.max(line, axis=1) + 1])

    residual, picked = outer_residual_and_gather(
        solution, source_term, permittivity, counts, near, y_rows, up, down, inner, inner_lines, own_line, own_depth
    )
    picked = picked.reshape(capacity, ns * block_rows).astype(jnp.bfloat16)
    everyone = lax.all_gather(to_all_wide(picked, wide_count), "narrow", axis=0, tiled=True)

    columns = jnp.take(everyone, held_at, axis=0)
    columns = columns.reshape(-1, ns, block_rows).transpose(1, 0, 2).reshape(ns, -1)
    parts, base = [], 0
    for inv in inverses:
        width = inv.shape[0] * inv.shape[2]
        parts.append(columns[:, base : base + width].reshape(ns, inv.shape[0], -1).transpose(1, 0, 2))
        base += width
    partial = fronts(parts, inverses).astype(jnp.bfloat16)
    rows = partial.shape[1] // block_rows
    shares = lax.all_gather(partial.reshape(ns, rows, block_rows), "narrow", axis=0, tiled=False)
    summed = jnp.sum(shares.astype(jnp.float32), axis=0).astype(jnp.bfloat16)
    summed = summed.transpose(1, 0, 2).reshape(rows, ns * block_rows)
    updates = to_all_wide(summed, wide_count)

    values = jnp.take(updates, near_rows.reshape(-1), axis=0).astype(jnp.float32)
    return tuple(correct(solution, residual, permittivity, loads, own_line, own_depth, line, depth, values))


def solution(mesh):
    return jax.shard_map(
        on_device,
        mesh=mesh,
        in_specs=(
            P(None, None, "wide", "narrow", None),
            P(None, None, "wide", "narrow", None),
            P("wide", "narrow", None),
            P("wide", "narrow"),
            P(None, "wide", "narrow"),
            P(None, "wide", "narrow"),
            P(),
            P(),
        ),
        out_specs=(P(None, None, "wide", "narrow", None), P(None, None, "wide", "narrow", None)),
        check_vma=False,
    )
```

time: 137 us -> 129 us (0.942)
  the two profiles are of different devices: /device:TPU:6 before, /device:TPU:3 now
where the time goes in v2:
time: 129 us
  Pallas kernels  65.7 us (51%)
  blocking collectives  23.9 us (19%)
  starting transfers between devices  13.4 us (10%)
  waiting for transfers between devices  9.27 us (7%)
  local copies, waits for them, and re-layouts  8.58 us (7%)
  other arithmetic  7.2 us (6%)
    pallas_call x1, Pallas kernels, correct(): pl.pallas_call(correct_kernel, grid_spec=grid_spec, out_shape=[jax.ShapeD...  23.3 us
    pallas_call x1, Pallas kernels, fronts(): pl.pallas_call(fronts_kernel, in_specs=[here] * 3 + [there] * 3, out_spec...  16.3 us
    pallas_call x1, Pallas kernels, outer_residual_and_gather(): pl.pallas_call(gather_kernel, grid_spec=grid_spec, out_shape=[jax.ShapeDt...  14.6 us
    all_gather x1, blocking collectives, on_device(): lax.all_gather(to_all_wide(picked, wide_count), 'narrow', axis=0, tiled=T...  10.6 us
    all_to_all x2, waiting for transfers between devices, to_all_wide(): return lax.all_to_all(spread, 'wide', 0, 0, tiled=True)  9.27 us
    all_to_all x2, starting transfers between devices, to_all_wide(): return lax.all_to_all(spread, 'wide', 0, 0, tiled=True)  8.17 us
    all_gather x1, blocking collectives, on_device(): y_rows = lax.all_gather(outer_rows(solution), 'narrow', axis=0, tiled=False)  7.82 us
    pallas_call x1, Pallas kernels, inner_residual(): pl.pallas_call(inner_kernel, grid_spec=grid_spec, out_shape=[jax.ShapeDty...  6.67 us
  transfers between devices with their start and end apart: 4, of which 2 were waited for; matrix products, arithmetic and copies ran while one was open for 6% of the time, Pallas kernels for 5%

profile of v2, /device:TPU:3, one launch (start us, length us, event | category | flops | bytes accessed | tf_op | source)
XLA Modules:
  0.0 129.3 jit_solution(9903500881492698476)
XLA Ops:
  0.7 2.0 %outer_rows.1 = bf16[2,5,8,384]{3,2,1,0:T(8,128)(2,1)} custom-call(f32[2,3,8,48,384]{4,3,2,1,0:T(8,128)} %sol_ref.5, f32[2,3,8,48,384]{4,3,2,1,0:T(8,128)} %sol_ref.5), custom_call_target="tpu_custom_call" | custom-call | tf_op jit(solution)/shard_map/outer_rows/pallas_call | solution.py:63
  2.6 7.8 %all-gather = bf16[8,5,8,384]{3,2,1,0:T(8,128)(2,1)} all-gather(bf16[2,5,8,384]{3,2,1,0:T(8,128)(2,1)} %outer_rows.1), channel_id=2, replica_groups=mesh['wide'=8,'narrow'=4] {'narrow'}, dimensions={0}, use_global_device_ids=true | all-gather | bytes 307200 | tf_op jit(solution)/shard_map/all_gather | solution.py:615
  11.1 2.9 %outer_planes.1 = (bf16[2,96,384]{2,1,0:T(8,128)(2,1)}, bf16[2,112,384]{2,1,0:T(8,128)(2,1)}) custom-call(s32[4]{0:T(128)} %pad_add_fusion.1.near_ref, f32[2,3,8,48,384]{4,3,2,1,0:T(8,128)} %sol_ref.5, f32[2,3,8,48,384]{4,3,2,1,0:T(8,128)} %sol_ref.5, bf16[4,2,5,8,384]{4,3,2,1,0:T(8,128)(2,1)} %bitcast.72, bf16[4,2,5,8,384]{4,3,2,1,0:T(8,128)(2,1)} %bitcast.73), custom_call_target="tpu_custom_call" | custom-call | tf_op jit(solution)/shard_map/outer_planes/pallas_call | solution.py:113
  14.0 3.2 %collective-permute-start = (bf16[2,96,384]{2,1,0:T(8,128)(2,1)}, bf16[2,96,384]{2,1,0:T(8,128)(2,1)S(1)}, u32[]{:S(2)}, u32[]{:S(2)}) collective-permute-start(bf16[2,96,384]{2,1,0:T(8,128)(2,1)} %get-tuple-element.8), channel_id=1, source_target_pairs={{0,4},{4,8},{8,12},{12,16},{16,20},{20,24},{24,28},{1,5},{5,9},{9,... | collective-permute-start | bytes 442376 | tf_op jit(solution)/shard_map/ppermute | solution.py:618
  17.2 2.1 %collective-permute-start.1 = (bf16[2,112,384]{2,1,0:T(8,128)(2,1)}, bf16[2,112,384]{2,1,0:T(8,128)(2,1)S(1)}, u32[]{:S(2)}, u32[]{:S(2)}) collective-permute-start(bf16[2,112,384]{2,1,0:T(8,128)(2,1)} %get-tuple-element.9), channel_id=1, source_target_pairs={{4,0},{8,4},{12,8},{16,12},{20,16},{24,20},{28,24},{5,1},{9,5},{13... | collective-permute-start | bytes 516104 | tf_op jit(solution)/shard_map/ppermute | solution.py:619
  20.3 0.7 gather_fusion
  23.6 6.7 %inner_residual.1 = (f32[2,3,8,48,384]{4,3,2,1,0:T(8,128)}, bf16[1152,768]{1,0:T(8,128)(2,1)}) custom-call(s32[4]{0:T(128)} %pad_add_fusion.1.near_ref, f32[2,3,8,48,384]{4,3,2,1,0:T(8,128)} %sol_ref.5, f32[2,3,8,48,384]{4,3,2,1,0:T(8,128)} %src_ref.3, bf16[8,48,384]{2,1,0:T(8,128)(2,1)} %perm_ref.5, bf16[4,2,5,8,384]{4,3,2,1,0:T(8,128)(2,1)} %bitcast.74, ...), custom_call_target="tpu_custom_call" | custom-call | flops 53084160 | bytes 12386304 | tf_op jit(solution)/shard_map/inner_residual/pallas_call | solution.py:244
  31.6 14.6 %outer_residual_gather.1 = (f32[2,3,8,48,384]{4,3,2,1,0:T(8,128)}, f32[4,8,256]{2,1,0:T(8,128)}) custom-call(s32[7]{0:T(128)} %copy-done.4, s32[4]{0:T(128)} %pad_add_fusion.1.near_ref, f32[2,3,8,48,384]{4,3,2,1,0:T(8,128)} %sol_ref.5, f32[2,3,8,48,384]{4,3,2,1,0:T(8,128)} %src_ref.3, ...), custom_call_target="tpu_custom_call", output_to_operand_aliasing={{0}: (12, {})} | custom-call | tf_op jit(solution)/shard_map/outer_residual_gather/pallas_call | solution.py:364
  46.3 0.8 convert_bitcast_fusion.1
  47.0 0.7 broadcast_in_dim.117
  47.7 3.3 %all-to-all-start = ((bf16[8,32,256]{2,1,0:T(8,128)(2,1)}), bf16[8,32,256]{2,1,0:T(8,128)(2,1)S(1)}, u32[]{:S(2)}, u32[]{:S(2)}) async-start(bf16[8,32,256]{2,1,0:T(8,128)(2,1)} %broadcast_in_dim.117), calls=%async_computation | async-start | bytes 262144 | tf_op jit(solution)/shard_map/all_to_all | solution.py:596
  51.5 3.6 %all-to-all-done = bf16[8,32,256]{2,1,0:T(8,128)(2,1)S(1)} async-done(((bf16[8,32,256]{2,1,0:T(8,128)(2,1)}), bf16[8,32,256]{2,1,0:T(8,128)(2,1)S(1)}, u32[]{:S(2)}, u32[]{:S(2)}) %all-to-all-start) | async-done | bytes 131104 | tf_op jit(solution)/shard_map/all_to_all | solution.py:596
  55.1 10.6 %all_gather.14 = bf16[1024,256]{1,0:T(8,128)(2,1)S(1)} all-gather(bf16[256,256]{1,0:T(8,128)(2,1)S(1)} %bitcast.81), channel_id=1, replica_groups=mesh['wide'=8,'narrow'=4] {'narrow'}, dimensions={0}, use_global_device_ids=true | all-gather | bytes 655360 | tf_op jit(solution)/shard_map/all_gather | solution.py:676
  65.8 0.8 gather_fusion.1
  68.0 16.3 %fronts.1 = f32[2,8192]{1,0:T(2,128)} custom-call(bf16[1,2,4096]{2,1,0:T(2,128)(2,1)} %get-tuple-element.29.x_top, bf16[2,2,2048]{2,1,0:T(2,128)(2,1)} %bitcast.85, bf16[4,2,2048]{2,1,0:T(2,128)(2,1)} %bitcast.84, bf16[1,2048,4096]{2,1,0:T(8,128)(2,1)} %bitcast.71, bf16[2,1024,2048]{2,1,0:T(8,128)(2,1)} %mid_ref.1, bf16[4,1024,2048]{2,1,0:T(8,128)(2,1)} %low_ref.3), custom_call_target="tpu_custom_call" | custom-call | flops 83886080 | bytes 41943040 | tf_op jit(solution)/shard_map/fronts/pallas_call | solution.py:404
  84.3 0.9 convert_bitcast_fusion
  85.2 5.4 %all_gather.15 = bf16[4,2,64,128]{3,2,1,0:T(8,128)(2,1)S(1)} all-gather(bf16[1,2,64,128]{3,2,1,0:T(8,128)(2,1)S(1)} %copy.34), channel_id=1, replica_groups=mesh['wide'=8,'narrow'=4] {'narrow'}, dimensions={0}, use_global_device_ids=true | all-gather | bytes 163840 | tf_op jit(solution)/shard_map/all_gather | solution.py:687
  90.7 0.7 broadcast_in_dim.121
  91.4 4.8 %all-to-all-start.1 = ((bf16[8,64,256]{2,1,0:T(8,128)(2,1)}), bf16[8,64,256]{2,1,0:T(8,128)(2,1)S(1)}, u32[]{:S(2)}, u32[]{:S(2)}) async-start(bf16[8,64,256]{2,1,0:T(8,128)(2,1)} %broadcast_in_dim.121), calls=%async_computation.1 | async-start | bytes 524288 | tf_op jit(solution)/shard_map/all_to_all | solution.py:596
  96.3 0.7 reshape.242.line_ref
  98.2 5.7 %all-to-all-done.1 = bf16[8,64,256]{2,1,0:T(8,128)(2,1)S(1)} async-done(((bf16[8,64,256]{2,1,0:T(8,128)(2,1)}), bf16[8,64,256]{2,1,0:T(8,128)(2,1)S(1)}, u32[]{:S(2)}, u32[]{:S(2)}) %all-to-all-start.1) | async-done | bytes 262176 | tf_op jit(solution)/shard_map/all_to_all | solution.py:596
  103.9 1.1 gather_fusion.2
  105.0 0.8 select_convert_fusion.value_ref
  105.8 23.3 %correct.1 = (f32[2,3,8,48,384]{4,3,2,1,0:T(8,128)}, f32[2,3,8,48,384]{4,3,2,1,0:T(8,128)}) custom-call(s32[55]{0:T(128)} %pad_add_fusion.count_ref, f32[2,3,8,48,384]{4,3,2,1,0:T(8,128)} %sol_ref.5, f32[2,3,8,48,384]{4,3,2,1,0:T(8,128)} %get-tuple-element.12.res_ref, bf16[8,48,384]{2,1,0:T(8,128)(2,1)} %perm_ref.5, s32[4,1024]{1,0:T(4,128)} %fusion.28.line_ref.own_line_ref, ...), custom_call_target="tpu_custom_call" | custom-call | tf_op jit(solution)/shard_map/correct/pallas_call | solution.py:563
  (83 shorter events, 8.7 us)
Async XLA Ops:
  0.6 19.7 %copy-start = (s32[512,128]{1,0:T(8,128)S(1)}, s32[512,128]{1,0:T(8,128)}, u32[]{:S(2)}) copy-start(s32[512,128]{1,0:T(8,128)} %param.20) | copy-start | bytes 786436
  11.1 8.2 %copy-start.3 = (s32[512,1]{0,1:T(1,128)S(1)}, s32[512,1]{0,1:T(1,128)}, u32[]{:S(2)}) copy-start(s32[512,1]{0,1:T(1,128)} %param.19) | copy-start | bytes 6148
  11.1 8.5 %copy-start.8 = (s32[7]{0:T(128)S(1)}, s32[7]{0:T(128)}, u32[]{:S(2)}) copy-start(s32[7]{0:T(128)} %constant.168.clone) | copy-start | bytes 88
  11.1 8.5 %copy-start.9 = (s32[7]{0:T(128)S(1)}, s32[7]{0:T(128)}, u32[]{:S(2)}) copy-start(s32[7]{0:T(128)} %constant.167.clone) | copy-start | bytes 88
  11.1 8.8 %copy-start.7 = (s32[512]{0:T(512)S(1)}, s32[512]{0:T(512)}, u32[]{:S(2)}) copy-start(s32[512]{0:T(512)} %constant.172) | copy-start | bytes 6148
  11.1 10.7 %copy-start.10 = (s32[4,1,1]{0,2,1:T(1,128)S(1)}, s32[4,1,1]{0,2,1:T(1,128)}, u32[]{:S(2)}) copy-start(s32[4,1,1]{0,2,1:T(1,128)} %constant.171.clone) | copy-start | bytes 52
  11.1 10.8 %copy-start.6 = (s32[4,128]{1,0:T(4,128)S(1)}, s32[4,128]{1,0:T(4,128)}, u32[]{:S(2)}) copy-start(s32[4,128]{1,0:T(4,128)} %constant.173) | copy-start | bytes 6148
  14.0 16.9 %collective-permute-start = (bf16[2,96,384]{2,1,0:T(8,128)(2,1)}, bf16[2,96,384]{2,1,0:T(8,128)(2,1)S(1)}, u32[]{:S(2)}, u32[]{:S(2)}) collective-permute-start(bf16[2,96,384]{2,1,0:T(8,128)(2,1)} %get-tuple-element.8), channel_id=1, source_target_pairs={{0,4},{4,8},{8,12},{12,16},{16,20},{20,24},{24,28},{1,5},{5,9},{9,... | collective-permute-start | bytes 442376 | tf_op jit(solution)/shard_map/ppermute | solution.py:618
  17.2 13.8 %collective-permute-start.1 = (bf16[2,112,384]{2,1,0:T(8,128)(2,1)}, bf16[2,112,384]{2,1,0:T(8,128)(2,1)S(1)}, u32[]{:S(2)}, u32[]{:S(2)}) collective-permute-start(bf16[2,112,384]{2,1,0:T(8,128)(2,1)} %get-tuple-element.9), channel_id=1, source_target_pairs={{4,0},{8,4},{12,8},{16,12},{20,16},{24,20},{28,24},{5,1},{9,5},{13... | collective-permute-start | bytes 516104 | tf_op jit(solution)/shard_map/ppermute | solution.py:619
  19.8 10.5 %copy-start.4 = (s32[7]{0:T(128)}, s32[7]{0:T(128)S(1)}, u32[]{:S(2)}) copy-start(s32[7]{0:T(128)S(1)} %convert_reduce_fusion.1.count_ref) | copy-start | bytes 88
  30.9 0.7 copy-start.2
  30.9 0.7 copy-start.1
  47.7 7.4 %all-to-all-start = ((bf16[8,32,256]{2,1,0:T(8,128)(2,1)}), bf16[8,32,256]{2,1,0:T(8,128)(2,1)S(1)}, u32[]{:S(2)}, u32[]{:S(2)}) async-start(bf16[8,32,256]{2,1,0:T(8,128)(2,1)} %broadcast_in_dim.117), calls=%async_computation | async-start | bytes 262144 | tf_op jit(solution)/shard_map/all_to_all | solution.py:596
  68.0 29.6 %copy-start.5 = (s32[7]{0:T(128)S(1)}, s32[7]{0:T(128)}, u32[]{:S(2)}) copy-start(s32[7]{0:T(128)} %copy-done.4) | copy-start | bytes 88
  91.4 12.5 %all-to-all-start.1 = ((bf16[8,64,256]{2,1,0:T(8,128)(2,1)}), bf16[8,64,256]{2,1,0:T(8,128)(2,1)S(1)}, u32[]{:S(2)}, u32[]{:S(2)}) async-start(bf16[8,64,256]{2,1,0:T(8,128)(2,1)} %broadcast_in_dim.121), calls=%async_computation.1 | async-start | bytes 524288 | tf_op jit(solution)/shard_map/all_to_all | solution.py:596

commit v3 on v2

--- a/solution.py
+++ b/solution.py
@@ -52,74 +52,65 @@
 
 def rows_kernel(low_ref, high_ref, out_ref):
     top = high_ref.shape[3] - 1
-    rows = [low_ref[0, 0, :, 0, :], low_ref[0, 2, :, 0, :], *(high_ref[0, c, :, top, :] for c in range(3))]
-    for n, row in enumerate(rows):
-        out_ref[0, n] = row.astype(out_ref.dtype)
+    for s in range(out_ref.shape[0]):
+        rows = [low_ref[s, 0, :, 0, :], low_ref[s, 2, :, 0, :], *(high_ref[s, c, :, top, :] for c in range(3))]
+        for n, row in enumerate(rows):
+            out_ref[s, n] = row.astype(out_ref.dtype)
 
 
 def outer_rows(field):
     ns, _, cx, cy, cz = field.shape
-    slab = (1, 3, cx, 8, cz)
+    slab = (ns, 3, cx, 8, cz)
     return pl.pallas_call(
         rows_kernel,
-        grid=(ns,),
+        grid=(1,),
         in_specs=[
-            pl.BlockSpec(slab, lambda s: (s, 0, 0, 0, 0)),
-            pl.BlockSpec(slab, lambda s: (s, 0, 0, cy // 8 - 1, 0)),
-        ],
-        out_specs=pl.BlockSpec((1, 5, cx, cz), lambda s: (s, 0, 0, 0)),
+            pl.BlockSpec(slab, lambda g: (0, 0, 0, 0, 0)),
+            pl.BlockSpec(slab, lambda g: (0, 0, 0, cy // 8 - 1, 0)),
+        ],
+        out_specs=pl.BlockSpec((ns, 5, cx, cz), lambda g: (0, 0, 0, 0)),
         out_shape=jax.ShapeDtypeStruct((ns, 5, cx, cz), jnp.bfloat16),
         compiler_params=pltpu.CompilerParams(vmem_limit_bytes=60 * MIB),
         name="outer_rows",
     )(field, field)
 
 
-def near_row(near_ref, side, ref, n, i):
-    row = ref[n].astype(jnp.float32)
-    return jnp.where(near_ref[2 + side] > 0, row[i : i + 1], 0.0)
-
-
-def planes_kernel(near_ref, first_ref, last_ref, prev_ref, next_ref, up_ref, down_ref):
-    planes = prev_ref.shape[3]
-    cy = first_ref.shape[3]
-    dtype = up_ref.dtype
-    ex, ey, ez = last_ref[0, 0, 0], last_ref[0, 1, 0], last_ref[0, 2, 0]
-    past = near_row(near_ref, 1, next_ref.at[0, 0], 0, planes - 1)
-    up_ref[0, :cy] = (ey + (ahead(ex, 0, past) - ex)).astype(dtype)
-    up_ref[0, cy:] = (ez + (ahead(ex, 1) - ex)).astype(dtype)
-    down_ref[0, :cy] = first_ref[0, 1, 0].astype(dtype)
-    down_ref[0, cy : 2 * cy] = first_ref[0, 2, 0].astype(dtype)
-    before = near_row(near_ref, 0, prev_ref.at[0, 0], 3, 0)
-    down_ref[0, 2 * cy :] = jnp.broadcast_to(before, (down_ref.shape[1] - 2 * cy, before.shape[1])).astype(dtype)
-
-
-def outer_planes(field, near, rows):
+def beside(rows_ref):
+    me, last = lax.axis_index("narrow"), rows_ref.shape[0] - 1
+    return (jnp.maximum(me - 1, 0), me > 0), (jnp.minimum(me + 1, last), me < last)
+
+
+def planes_kernel(first_ref, last_ref, rows_ref, up_ref, down_ref):
+    planes, cy, dtype = rows_ref.shape[3], first_ref.shape[3], up_ref.dtype
+    (before, has_before), (after, has_after) = beside(rows_ref)
+    for s in range(up_ref.shape[0]):
+        ex, ey, ez = (last_ref[s, c, 0] for c in range(3))
+        past = jnp.where(has_after, rows_ref[after, s, 0].astype(jnp.float32)[planes - 1 :], 0.0)
+        up_ref[s, :cy] = (ey + (ahead(ex, 0, past) - ex)).astype(dtype)
+        up_ref[s, cy:] = (ez + (ahead(ex, 1) - ex)).astype(dtype)
+        down_ref[s, :cy] = first_ref[s, 1, 0].astype(dtype)
+        down_ref[s, cy : 2 * cy] = first_ref[s, 2, 0].astype(dtype)
+        edge = jnp.where(has_before, rows_ref[before, s, 3].astype(jnp.float32)[:1], 0.0)
+        down_ref[s, 2 * cy :] = jnp.broadcast_to(edge, (down_ref.shape[1] - 2 * cy, edge.shape[1])).astype(dtype)
+
+
+def outer_planes(field, rows):
     ns, _, cx, cy, cz = field.shape
-    plane = (1, 3, 1, cy, cz)
-    grid_spec = pltpu.PrefetchScalarGridSpec(
-        num_scalar_prefetch=1,
-        grid=(ns,),
-        in_specs=[
-            pl.BlockSpec(plane, lambda s, _: (s, 0, 0, 0, 0)),
-            pl.BlockSpec(plane, lambda s, _: (s, 0, cx - 1, 0, 0)),
-            pl.BlockSpec((1, 1, 5, cx, cz), lambda s, near: (near[0], s, 0, 0, 0)),
-            pl.BlockSpec((1, 1, 5, cx, cz), lambda s, near: (near[1], s, 0, 0, 0)),
-        ],
-        out_specs=[
-            pl.BlockSpec((1, 2 * cy, cz), lambda s, _: (s, 0, 0)),
-            pl.BlockSpec((1, 2 * cy + 16, cz), lambda s, _: (s, 0, 0)),
-        ],
-    )
+    plane = (ns, 3, 1, cy, cz)
+    heights = (2 * cy, 2 * cy + 16)
     return pl.pallas_call(
         planes_kernel,
-        grid_spec=grid_spec,
-        out_shape=[
-            jax.ShapeDtypeStruct((ns, 2 * cy, cz), jnp.bfloat16),
-            jax.ShapeDtypeStruct((ns, 2 * cy + 16, cz), jnp.bfloat16),
-        ],
+        grid=(1,),
+        in_specs=[
+            pl.BlockSpec(plane, lambda g: (0, 0, 0, 0, 0)),
+            pl.BlockSpec(plane, lambda g: (0, 0, cx - 1, 0, 0)),
+            pl.BlockSpec(rows.shape, lambda g: (0,) * 5),
+        ],
+        out_specs=[pl.BlockSpec((ns, h, cz), lambda g: (0, 0, 0)) for h in heights],
+        out_shape=[jax.ShapeDtypeStruct((ns, h, cz), jnp.bfloat16) for h in heights],
         compiler_params=pltpu.CompilerParams(vmem_limit_bytes=60 * MIB),
         name="outer_planes",
-    )(near, field, field, rows, rows)
+    )(field, field, rows)
 
 
 def curl_plane(own, beyond, back_z, back_y, y_row_x, y_row_z, y_edge_z, y_edge_x):
@@ -138,11 +129,12 @@
     return (beyond[0] - ey) - (ahead(ex, 0, row_x) - ex), (ahead(ex, 1) - ex) - (beyond[1] - ez)
 
 
-def spread_rows(near_ref, prev_ref, next_ref, scratch):
+def spread_rows(rows_ref, scratch):
+    before, after = beside(rows_ref)
     for s in range(scratch.shape[0]):
         for n in range(5):
-            side, ref = (1, next_ref) if n < 2 else (0, prev_ref)
-            scratch[s, n] = jnp.where(near_ref[2 + side] > 0, ref[0, s, n].astype(jnp.float32), 0.0)
+            tile, there = after if n < 2 else before
+            scratch[s, n] = jnp.where(there, rows_ref[tile, s, n].astype(jnp.float32), 0.0)
 
 
 def residual_plane(s, i, own, beyond, back, rows, after, planes, at, scaled, lines):
@@ -161,7 +153,7 @@
 
 
 def inner_kernel(
-    near_ref, sol_ref, src_ref, perm_ref, prev_ref, over_ref, res_ref, out_ref,
+    sol_ref, src_ref, perm_ref, rows_ref, res_ref, out_ref,
     field, planes, lines, back_z, back_y, rows, field_sem, plane_sem, res_sem, line_sem,
 ):
     ns, _, cx, cy, _ = field.shape
@@ -183,7 +175,7 @@
         field_copy(i).start()
         if 0 < i < cx - 1:
             plane_copy(i).start()
-    spread_rows(near_ref, prev_ref, over_ref, rows)
+    spread_rows(rows_ref, rows)
     field_copy(0).wait()
     field_copy(1).wait()
     for s in range(ns):
@@ -212,20 +204,17 @@
             line_copy(i, c).wait()
 
 
-def inner_residual(field, source, permittivity, near, y_rows):
+def inner_residual(field, source, permittivity, y_rows):
     ns, _, cx, cy, cz = field.shape
-    tile_rows = (1, ns, 5, cx, cz)
     anywhere = pl.BlockSpec(memory_space=pl.ANY)
     dma = pltpu.SemaphoreType.DMA
-    grid_spec = pltpu.PrefetchScalarGridSpec(
-        num_scalar_prefetch=1,
+    grid_spec = pl.GridSpec(
         grid=(1,),
         in_specs=[
             anywhere,
             anywhere,
-            pl.BlockSpec((cx, cy, cz), lambda g, _: (0, 0, 0)),
-            pl.BlockSpec(tile_rows, lambda g, near: (near[0], 0, 0, 0, 0)),
-            pl.BlockSpec(tile_rows, lambda g, near: (near[1], 0, 0, 0, 0)),
+            pl.BlockSpec((cx, cy, cz), lambda g: (0, 0, 0)),
+            pl.BlockSpec(y_rows.shape, lambda g: (0,) * 5),
         ],
         out_specs=[anywhere, anywhere],
         scratch_shapes=[
@@ -251,12 +240,12 @@
         compiler_params=pltpu.CompilerParams(vmem_limit_bytes=60 * MIB),
         cost_estimate=pl.CostEstimate(flops=60 * field.size, bytes_accessed=14 * field.size, transcendentals=0),
         name="inner_residual",
-    )(near, field, source, permittivity, y_rows, y_rows)
+    )(field, source, permittivity, y_rows)
 
 
 def gather_kernel(
-    count_ref, near_ref, sol_ref, src_ref, perm_ref, prev_ref, over_ref, up_ref, down_ref, inner_ref, line_ref, depth_ref, _,
-    res_ref, out_ref, field, planes, lines, turned, rows, field_sem, plane_sem, line_sem,
+    count_ref, sol_ref, src_ref, perm_ref, rows_ref, up_ref, down_ref, inner_ref, line_ref, depth_ref, _,
+    res_ref, out_ref, field, planes, lines, turned, rows, got_ref, field_sem, plane_sem, line_sem,
 ):
     ns, _, cx, cy, cz = sol_ref.shape
     total = lines.shape[0]
@@ -278,8 +267,8 @@
     ]
     for copy in field_copies[:2] + plane_copies[:1] + field_copies[2:] + plane_copies[1:] + line_copies:
         copy.start()
-    spread_rows(near_ref, prev_ref, over_ref, rows)
-    out_ref[...] = jnp.zeros_like(out_ref)
+    spread_rows(rows_ref, rows)
+    got_ref[...] = jnp.zeros_like(got_ref)
 
     for copy in field_copies[:2] + plane_copies[:1]:
         copy.wait()
@@ -309,7 +298,7 @@
             turned[b * 128 : (b + 1) * 128, a * 128 : (a + 1) * 128] = lines[
                 a * 128 : (a + 1) * 128, b * 128 : (b + 1) * 128
             ].T
-    group, width = out_ref.shape[1], line_ref.shape[1]
+    group, width = got_ref.shape[1], line_ref.shape[1]
 
     @pl.loop(0, pl.cdiv(count_ref[0], group))
     def _(p):
@@ -319,29 +308,30 @@
         for s in range(ns):
             sums = jnp.sum(jnp.where(at, got[s * cz : (s + 1) * cz], 0.0), axis=0, keepdims=True)
             for h in range(group):
-                out_ref[p, h : h + 1, s * 128 : (s + 1) * 128] = sums[:, h * 128 : (h + 1) * 128]
-
+                got_ref[p, h : h + 1, s * 128 : (s + 1) * 128] = sums[:, h * 128 : (h + 1) * 128]
+
+    picked = got_ref[...].reshape(out_ref.shape[1:]).astype(out_ref.dtype)
+    for w in range(out_ref.shape[0]):
+        out_ref[w] = picked
     for copy in res_copies:
         copy.wait()
 
 
-def outer_residual_and_gather(field, source, permittivity, counts, near, y_rows, up, down, residual, inner, line, depth):
+def outer_residual_and_gather(copies, field, source, permittivity, counts, y_rows, up, down, residual, inner, line, depth):
     ns, _, cx, cy, cz = field.shape
     total = 3 * cx * cy
     groups, group = line.shape[0], line.shape[1] // 128
     whole = lambda x: pl.BlockSpec(x.shape, lambda g, *_: (0,) * x.ndim)
-    tile_rows = (1, ns, 5, cx, cz)
     anywhere = pl.BlockSpec(memory_space=pl.ANY)
     dma = pltpu.SemaphoreType.DMA
     grid_spec = pltpu.PrefetchScalarGridSpec(
-        num_scalar_prefetch=2,
+        num_scalar_prefetch=1,
         grid=(1,),
         in_specs=[
             anywhere,
             anywhere,
             whole(permittivity),
-            pl.BlockSpec(tile_rows, lambda g, _, near: (near[0], 0, 0, 0, 0)),
-            pl.BlockSpec(tile_rows, lambda g, _, near: (near[1], 0, 0, 0, 0)),
+            whole(y_rows),
             whole(up),
             whole(down),
             anywhere,
@@ -349,13 +339,14 @@
             whole(depth),
             anywhere,
         ],
-        out_specs=[anywhere, pl.BlockSpec((groups, group, ns * 128), lambda g, *_: (0, 0, 0))],
+        out_specs=[anywhere, pl.BlockSpec((copies, groups * group, ns * 128), lambda g, *_: (0, 0, 0))],
         scratch_shapes=[
             pltpu.VMEM((ns, 3, 4, cy, cz), jnp.float32),
             pltpu.VMEM((ns, 3, 2, cy, cz), jnp.float32),
             pltpu.VMEM((total, ns * cz), jnp.bfloat16),
             pltpu.VMEM((ns * cz, total), jnp.bfloat16),
             pltpu.VMEM((ns, 5, cx, cz), jnp.float32),
+            pltpu.VMEM((groups, group, ns * 128), jnp.float32),
             dma((4,)),
             dma((2,)),
             dma((3,)),
@@ -366,17 +357,18 @@
         grid_spec=grid_spec,
         out_shape=[
             jax.ShapeDtypeStruct(field.shape, jnp.float32),
-            jax.ShapeDtypeStruct((groups, group, ns * 128), jnp.float32),
-        ],
-        input_output_aliases={12: 0},
+            jax.ShapeDtypeStruct((copies, groups * group, ns * 128), jnp.bfloat16),
+        ],
+        input_output_aliases={10: 0},
         compiler_params=pltpu.CompilerParams(vmem_limit_bytes=60 * MIB),
         name="outer_residual_gather",
-    )(counts, near, field, source, permittivity, y_rows, y_rows, up, down, inner, line, depth, residual)
-
-
-def fronts_kernel(x_top, x_mid, x_low, top_ref, mid_ref, low_ref, y_ref, top_buf, mid_buf, low_buf, sem):
-    jobs, base = [], 0
-    for x_ref, w_ref, buf in ((x_top, top_ref, top_buf), (x_mid, mid_ref, mid_buf), (x_low, low_ref, low_buf)):
+    )(counts, field, source, permittivity, y_rows, up, down, inner, line, depth, residual)
+
+
+def fronts_kernel(columns_ref, top_ref, mid_ref, low_ref, y_ref, top_buf, mid_buf, low_buf, x_buf, y_buf, sem):
+    ns = y_buf.shape[0]
+    jobs, base, column = [], 0, 0
+    for w_ref, buf in ((top_ref, top_buf), (mid_ref, mid_buf), (low_ref, low_buf)):
         count, height, width = w_ref.shape
         rows = height
         while rows > 256 and rows * width * 2 > 4 * MIB:
@@ -385,37 +377,54 @@
             for r in range(0, height, rows):
                 at = pl.ds(r, rows)
                 copy = pltpu.make_async_copy(w_ref.at[f, at], buf.at[f, at], sem.at[len(jobs)])
-                jobs.append((copy, x_ref, buf, f, at, pl.ds(base + r, rows)))
+                jobs.append((copy, buf, f, at, slice(column, column + width), (base + r) // 128))
             base += height
+            column += width
     for job in jobs:
         job[0].start()
-    for copy, x_ref, buf, f, at, out in jobs:
+    columns = columns_ref[...].astype(jnp.float32)
+    for b in range(columns.shape[0]):
+        for s in range(ns):
+            x_buf[s : s + 1, b * 128 : (b + 1) * 128] = columns[b : b + 1, s * 128 : (s + 1) * 128]
+    for copy, buf, f, at, lanes, first in jobs:
         copy.wait()
-        y_ref[:, out] = lax.dot_general(
-            x_ref[f], buf[f, at], (((1,), (1,)), ((), ())), preferred_element_type=jnp.float32
+        got = lax.dot_general(
+            x_buf[:, lanes].astype(jnp.bfloat16),
+            buf[f, at],
+            (((1,), (1,)), ((), ())),
+            preferred_element_type=jnp.float32,
         )
-
-
-def fronts(parts, inverses):
-    sources = parts[0].shape[1]
-    height = sum(inv.shape[0] * inv.shape[1] for inv in inverses)
+        for b in range(got.shape[1] // 128):
+            for s in range(ns):
+                y_buf[s, first + b : first + b + 1] = got[s : s + 1, b * 128 : (b + 1) * 128]
+    y_ref[...] = y_buf[...].astype(y_ref.dtype)
+
+
+def fronts(columns, inverses):
+    ns = columns.shape[1] // 128
+    blocks = sum(inv.shape[0] * inv.shape[1] for inv in inverses) // 128
     entries = sum(inv.size for inv in inverses)
     here, there = pl.BlockSpec(memory_space=pltpu.VMEM), pl.BlockSpec(memory_space=pl.ANY)
     return pl.pallas_call(
         fronts_kernel,
-        in_specs=[here] * 3 + [there] * 3,
+        in_specs=[here] + [there] * 3,
         out_specs=here,
-        out_shape=jax.ShapeDtypeStruct((sources, height), jnp.float32),
-        scratch_shapes=[pltpu.VMEM(inv.shape, inv.dtype) for inv in inverses] + [pltpu.SemaphoreType.DMA((64,))],
+        out_shape=jax.ShapeDtypeStruct((ns, blocks, 128), jnp.bfloat16),
+        scratch_shapes=[
+            *[pltpu.VMEM(inv.shape, inv.dtype) for inv in inverses],
+            pltpu.VMEM((ns, columns.shape[0] * 128), jnp.float32),
+            pltpu.VMEM((ns, blocks, 128), jnp.float32),
+            pltpu.SemaphoreType.DMA((64,)),
+        ],
         compiler_params=pltpu.CompilerParams(vmem_limit_bytes=60 * MIB),
         cost_estimate=pl.CostEstimate(flops=4 * entries, bytes_accessed=2 * entries, transcendentals=0),
         name="fronts",
-    )(*parts, *inverses)
+    )(columns, *inverses)
 
 
 def correct_kernel(
-    count_ref, sol_ref, res_ref, perm_ref, own_line_ref, own_depth_ref, line_ref, depth_ref, value_ref,
-    out_ref, new_ref, field, residual, delta, x_halo, y_halo, back_z, back_y, in_sem, out_sem,
+    count_ref, sol_ref, res_ref, perm_ref, own_line_ref, own_depth_ref, line_ref, depth_ref, given_ref,
+    out_ref, new_ref, value_ref, field, residual, delta, x_halo, y_halo, back_z, back_y, in_sem, out_sem,
 ):
     ns, _, planes, cy, cz = sol_ref.shape
     f32, half = jnp.float32, jnp.bfloat16
@@ -444,6 +453,7 @@
     def times(a, b):
         return lax.dot_general(a, b, (((1,), (1,)), ((), ())), preferred_element_type=f32)
 
+    value_ref[...] = given_ref[...].astype(f32)
     x_halo[...] = jnp.zeros_like(x_halo)
     y_halo[...] = jnp.zeros_like(y_halo)
     own_width = own_line_ref.shape[1]
@@ -549,6 +559,7 @@
         ],
         out_specs=[anywhere, anywhere],
         scratch_shapes=[
+            pltpu.VMEM(values.shape, jnp.float32),
             pltpu.VMEM(field.shape, jnp.float32),
             pltpu.VMEM(field.shape, jnp.float32),
             pltpu.VMEM((3 * cx * cy, ns * cz), jnp.float32),
@@ -604,20 +615,12 @@
     capacity = max(2, 2 * block_count // (wide_count * narrow_count))
     inverses = (inv_top[None], inv_mid, inv_low)
 
-    near = jnp.stack(
-        [
-            jnp.maximum(my_narrow - 1, 0),
-            jnp.minimum(my_narrow + 1, narrow_count - 1),
-            (my_narrow > 0).astype(jnp.int32),
-            (my_narrow < narrow_count - 1).astype(jnp.int32),
-        ]
-    )
     y_rows = lax.all_gather(outer_rows(solution), "narrow", axis=0, tiled=False)
-    to_up, to_down = outer_planes(solution, near, y_rows)
+    to_up, to_down = outer_planes(solution, y_rows)
     steps = [(w, w + 1) for w in range(wide_count - 1)]
     up = lax.ppermute(to_up, "wide", steps)
     down = lax.ppermute(to_down, "wide", [(b, a) for a, b in steps])
-    inner, inner_lines = inner_residual(solution, source_term, permittivity, near, y_rows)
+    inner, inner_lines = inner_residual(solution, source_term, permittivity, y_rows)
 
     block_tile = sep_tile[:, 0]
     block_ids = jnp.arange(block_count, dtype=jnp.int32)
@@ -640,7 +643,7 @@
         jnp.where(match, block_rows_of(inverses, wide_count, block_rows)[None, None, :], 0), axis=2
     )
     found = slots[None, :] < counts[:, None]
-    cells = jnp.take(sep_cell, near_ids.reshape(-1), axis=0).reshape(len(NEAR), capacity, block_rows)
+    cells = sep_cell.at[near_ids.reshape(-1)].get(mode="promise_in_bounds").reshape(len(NEAR), capacity, block_rows)
     depth = cells % cz
     row = cells // cz
     part, at_i, at_j = row // (cx * cy), row // cy % cx, row % cy
@@ -670,26 +673,19 @@
     loads = jnp.concatenate([counts, jnp.max(line, axis=1) + 1])
 
     residual, picked = outer_residual_and_gather(
-        solution, source_term, permittivity, counts, near, y_rows, up, down, inner, inner_lines, own_line, own_depth
-    )
-    picked = picked.reshape(capacity, ns * block_rows).astype(jnp.bfloat16)
-    everyone = lax.all_gather(to_all_wide(picked, wide_count), "narrow", axis=0, tiled=True)
-
-    columns = jnp.take(everyone, held_at, axis=0)
-    columns = columns.reshape(-1, ns, block_rows).transpose(1, 0, 2).reshape(ns, -1)
-    parts, base = [], 0
-    for inv in inverses:
-        width = inv.shape[0] * inv.shape[2]
-        parts.append(columns[:, base : base + width].reshape(ns, inv.shape[0], -1).transpose(1, 0, 2))
-        base += width
-    partial = fronts(parts, inverses).astype(jnp.bfloat16)
-    rows = partial.shape[1] // block_rows
-    shares = lax.all_gather(partial.reshape(ns, rows, block_rows), "narrow", axis=0, tiled=False)
+        wide_count, solution, source_term, permittivity, counts, y_rows, up, down, inner, inner_lines, own_line, own_depth
+    )
+    column = lax.all_to_all(picked.reshape(-1, ns * block_rows), "wide", 0, 0, tiled=True)
+    everyone = lax.all_gather(column, "narrow", axis=0, tiled=True)
+    columns = everyone.at[held_at].get(mode="promise_in_bounds")
+    partial = fronts(columns, inverses)
+    rows = partial.shape[1]
+    shares = lax.all_gather(partial, "narrow", axis=0, tiled=False)
     summed = jnp.sum(shares.astype(jnp.float32), axis=0).astype(jnp.bfloat16)
     summed = summed.transpose(1, 0, 2).reshape(rows, ns * block_rows)
     updates = to_all_wide(summed, wide_count)
 
-    values = jnp.take(updates, near_rows.reshape(-1), axis=0).astype(jnp.float32)
+    values = updates.at[near_rows.reshape(-1)].get(mode="promise_in_bounds")
     return tuple(correct(solution, residual, permittivity, loads, own_line, own_depth, line, depth, values))
 
 

time: 129 us -> 123 us (0.953)
  the two profiles are of different devices: /device:TPU:3 before, /device:TPU:27 now
where the time goes in v3:
time: 123 us; the launch traced here: 121 us
  Pallas kernels  60.8 us (49%)
  blocking collectives  20.9 us (17%)
  starting transfers between devices  16.8 us (14%)
  waiting for transfers between devices  9.67 us (8%)
  local copies, waits for them, and re-layouts  7.75 us (6%)
  other arithmetic  3.9 us (3%)
    pallas_call x1, Pallas kernels, correct(): pl.pallas_call(correct_kernel, grid_spec=grid_spec, out_shape=[jax.ShapeD...  19.6 us
    pallas_call x1, Pallas kernels, fronts(): pl.pallas_call(fronts_kernel, in_specs=[here] + [there] * 3, out_specs=he...  16.3 us
    pallas_call x1, Pallas kernels, outer_residual_and_gather(): pl.pallas_call(gather_kernel, grid_spec=grid_spec, out_shape=[jax.ShapeDt...  14.8 us
    all_gather x1, blocking collectives, on_device(): y_rows = lax.all_gather(outer_rows(solution), 'narrow', axis=0, tiled=False)  7.82 us
    all_gather x1, blocking collectives, on_device(): everyone = lax.all_gather(column, 'narrow', axis=0, tiled=True)  7.46 us
    pallas_call x1, Pallas kernels, inner_residual(): pl.pallas_call(inner_kernel, grid_spec=grid_spec, out_shape=[jax.ShapeDty...  6.08 us
    all_to_all x1, starting transfers between devices, to_all_wide(): return lax.all_to_all(spread, 'wide', 0, 0, tiled=True)  5.92 us
    all_gather x1, blocking collectives, on_device(): shares = lax.all_gather(partial, 'narrow', axis=0, tiled=False)  5.63 us
  transfers between devices with their start and end apart: 4, of which 2 were waited for; matrix products, arithmetic and copies ran while one was open for 6% of the time, Pallas kernels for 5%

profile of v3, /device:TPU:27, one launch (start us, length us, event | category | flops | bytes accessed | tf_op | source)
XLA Modules:
  0.0 121.0 jit_solution(18181213813056633132)
XLA Ops:
  0.6 2.0 %outer_rows.1 = bf16[2,5,8,384]{3,2,1,0:T(8,128)(2,1)} custom-call(f32[2,3,8,48,384]{4,3,2,1,0:T(8,128)} %sol_ref.5, f32[2,3,8,48,384]{4,3,2,1,0:T(8,128)} %sol_ref.5), custom_call_target="tpu_custom_call" | custom-call | tf_op jit(solution)/shard_map/outer_rows/pallas_call | solution.py:64
  2.7 7.8 %all-gather = bf16[8,5,8,384]{3,2,1,0:T(8,128)(2,1)} all-gather(bf16[2,5,8,384]{3,2,1,0:T(8,128)(2,1)} %outer_rows.1), channel_id=2, replica_groups=mesh['wide'=8,'narrow'=4] {'narrow'}, dimensions={0}, use_global_device_ids=true | all-gather | bytes 307200 | tf_op jit(solution)/shard_map/all_gather | solution.py:618
  10.5 2.0 %outer_planes.1 = (bf16[2,96,384]{2,1,0:T(8,128)(2,1)}, bf16[2,112,384]{2,1,0:T(8,128)(2,1)}) custom-call(f32[2,3,8,48,384]{4,3,2,1,0:T(8,128)} %sol_ref.5, f32[2,3,8,48,384]{4,3,2,1,0:T(8,128)} %sol_ref.5, bf16[4,2,5,8,384]{4,3,2,1,0:T(8,128)(2,1)} %bitcast.43), custom_call_target="tpu_custom_call" | custom-call | tf_op jit(solution)/shard_map/outer_planes/pallas_call | solution.py:101
  12.6 1.4 %collective-permute-start = (bf16[2,96,384]{2,1,0:T(8,128)(2,1)}, bf16[2,96,384]{2,1,0:T(8,128)(2,1)S(1)}, u32[]{:S(2)}, u32[]{:S(2)}) collective-permute-start(bf16[2,96,384]{2,1,0:T(8,128)(2,1)} %get-tuple-element.8), channel_id=1, source_target_pairs={{0,4},{4,8},{8,12},{12,16},{16,20},{20,24},{24,28},{1,5},{5,9},{9,... | collective-permute-start | bytes 442376 | tf_op jit(solution)/shard_map/ppermute | solution.py:621
  14.0 4.0 %collective-permute-start.1 = (bf16[2,112,384]{2,1,0:T(8,128)(2,1)}, bf16[2,112,384]{2,1,0:T(8,128)(2,1)S(1)}, u32[]{:S(2)}, u32[]{:S(2)}) collective-permute-start(bf16[2,112,384]{2,1,0:T(8,128)(2,1)} %get-tuple-element.9), channel_id=1, source_target_pairs={{4,0},{8,4},{12,8},{16,12},{20,16},{24,20},{28,24},{5,1},{9,5},{13... | collective-permute-start | bytes 516104 | tf_op jit(solution)/shard_map/ppermute | solution.py:622
  19.0 0.7 gather_fusion
  21.2 0.6 fusion.26.line_ref.own_line_ref
  21.8 0.6 reshape_squeeze.3.depth_ref.own_depth_ref
  22.8 6.1 %inner_residual.1 = (f32[2,3,8,48,384]{4,3,2,1,0:T(8,128)}, bf16[1152,768]{1,0:T(8,128)(2,1)}) custom-call(f32[2,3,8,48,384]{4,3,2,1,0:T(8,128)} %sol_ref.5, f32[2,3,8,48,384]{4,3,2,1,0:T(8,128)} %src_ref.3, bf16[8,48,384]{2,1,0:T(8,128)(2,1)} %perm_ref.5, bf16[4,2,5,8,384]{4,3,2,1,0:T(8,128)(2,1)} %bitcast.44), custom_call_target="tpu_custom_call" | custom-call | flops 53084160 | bytes 12386304 | tf_op jit(solution)/shard_map/inner_residual/pallas_call | solution.py:233
  29.3 0.6 copy-done.2
  30.0 14.8 %outer_residual_gather.1 = (f32[2,3,8,48,384]{4,3,2,1,0:T(8,128)}, bf16[8,32,256]{2,1,0:T(8,128)(2,1)}) custom-call(s32[7]{0:T(128)} %copy-done.4, f32[2,3,8,48,384]{4,3,2,1,0:T(8,128)} %sol_ref.5, f32[2,3,8,48,384]{4,3,2,1,0:T(8,128)} %src_ref.3, bf16[8,48,384]{2,1,0:T(8,128)(2,1)} %perm_ref.5, ...), custom_call_target="tpu_custom_call", output_to_operand_aliasing={{0}: (10, {})} | custom-call | tf_op jit(solution)/shard_map/outer_residual_gather/pallas_call | solution.py:355
  44.7 5.4 %all-to-all-start = ((bf16[8,32,256]{2,1,0:T(8,128)(2,1)}), bf16[8,32,256]{2,1,0:T(8,128)(2,1)S(1)}, u32[]{:S(2)}, u32[]{:S(2)}) async-start(bf16[8,32,256]{2,1,0:T(8,128)(2,1)} %get-tuple-element.13), calls=%async_computation | async-start | bytes 262144 | tf_op jit(solution)/shard_map/all_to_all | solution.py:678
  50.2 4.4 %all-to-all-done = bf16[8,32,256]{2,1,0:T(8,128)(2,1)S(1)} async-done(((bf16[8,32,256]{2,1,0:T(8,128)(2,1)}), bf16[8,32,256]{2,1,0:T(8,128)(2,1)S(1)}, u32[]{:S(2)}, u32[]{:S(2)}) %all-to-all-start) | async-done | bytes 131104 | tf_op jit(solution)/shard_map/all_to_all | solution.py:678
  54.6 7.5 %all_gather.17 = bf16[1024,256]{1,0:T(8,128)(2,1)S(1)} all-gather(bf16[256,256]{1,0:T(8,128)(2,1)S(1)} %bitcast.48), channel_id=1, replica_groups=mesh['wide'=8,'narrow'=4] {'narrow'}, dimensions={0}, use_global_device_ids=true | all-gather | bytes 655360 | tf_op jit(solution)/shard_map/all_gather | solution.py:679
  62.1 1.5 %gather_fusion.1 = bf16[128,256]{1,0:T(8,128)(2,1)} fusion(bf16[1024,256]{1,0:T(8,128)(2,1)S(1)} %all_gather.17, s32[1024]{0:T(1024)S(1)} %pad_clamp_fusion.1), kind=kCustom, calls=%fused_computation.1 | custom fusion | bytes 131584 | tf_op jit(solution)/shard_map/gather | solution.py:680
  63.6 16.3 %fronts.1 = bf16[2,64,128]{2,1,0:T(8,128)(2,1)} custom-call(bf16[128,256]{1,0:T(8,128)(2,1)} %gather_fusion.1, bf16[1,2048,4096]{2,1,0:T(8,128)(2,1)} %bitcast.41, bf16[2,1024,2048]{2,1,0:T(8,128)(2,1)} %mid_ref.1, bf16[4,1024,2048]{2,1,0:T(8,128)(2,1)} %low_ref.3), custom_call_target="tpu_custom_call" | custom-call | flops 83886080 | bytes 41943040 | tf_op jit(solution)/shard_map/fronts/pallas_call | solution.py:408
  79.9 5.6 %all-gather.1 = bf16[8,64,128]{2,1,0:T(8,128)(2,1)S(1)} all-gather(bf16[2,64,128]{2,1,0:T(8,128)(2,1)} %fronts.1), channel_id=3, replica_groups=mesh['wide'=8,'narrow'=4] {'narrow'}, dimensions={0}, use_global_device_ids=true | all-gather | bytes 163840 | tf_op jit(solution)/shard_map/all_gather | solution.py:683
  85.5 0.7 broadcast_in_dim.80
  86.2 5.9 %all-to-all-start.1 = ((bf16[8,64,256]{2,1,0:T(8,128)(2,1)}), bf16[8,64,256]{2,1,0:T(8,128)(2,1)S(1)}, u32[]{:S(2)}, u32[]{:S(2)}) async-start(bf16[8,64,256]{2,1,0:T(8,128)(2,1)} %broadcast_in_dim.80), calls=%async_computation.1 | async-start | bytes 524288 | tf_op jit(solution)/shard_map/all_to_all | solution.py:607
  92.2 0.7 reshape.203.line_ref
  92.9 0.7 reshape.204.depth_ref
  94.2 5.2 %all-to-all-done.1 = bf16[8,64,256]{2,1,0:T(8,128)(2,1)S(1)} async-done(((bf16[8,64,256]{2,1,0:T(8,128)(2,1)}), bf16[8,64,256]{2,1,0:T(8,128)(2,1)S(1)}, u32[]{:S(2)}, u32[]{:S(2)}) %all-to-all-start.1) | async-done | bytes 262176 | tf_op jit(solution)/shard_map/all_to_all | solution.py:607
  99.4 1.7 %gather_fusion.2 = bf16[224,256]{1,0:T(8,128)(2,1)} fusion(bf16[512,256]{1,0:T(8,128)(2,1)S(1)} %bitcast.42, s32[1024]{0:T(1024)S(1)} %pad_clamp_fusion), kind=kCustom, calls=%fused_computation.2 | custom fusion | bytes 230272 | tf_op jit(solution)/shard_map/gather | solution.py:688
  101.1 19.6 %correct.1 = (f32[2,3,8,48,384]{4,3,2,1,0:T(8,128)}, f32[2,3,8,48,384]{4,3,2,1,0:T(8,128)}) custom-call(s32[55]{0:T(128)} %pad_add_fusion.count_ref, f32[2,3,8,48,384]{4,3,2,1,0:T(8,128)} %sol_ref.5, f32[2,3,8,48,384]{4,3,2,1,0:T(8,128)} %get-tuple-element.12.res_ref, bf16[8,48,384]{2,1,0:T(8,128)(2,1)} %perm_ref.5, s32[4,1024]{1,0:T(4,128)} %fusion.26.line_ref.own_line_ref, ...), custom_call_target="tpu_custom_call" | custom-call | tf_op jit(solution)/shard_map/correct/pallas_call | solution.py:574
  (71 shorter events, 3.9 us)
Async XLA Ops:
  0.6 18.4 %copy-start = (s32[512,128]{1,0:T(8,128)S(1)}, s32[512,128]{1,0:T(8,128)}, u32[]{:S(2)}) copy-start(s32[512,128]{1,0:T(8,128)} %param.20) | copy-start | bytes 786436
  10.5 7.5 %copy-start.3 = (s32[512,1]{0,1:T(1,128)S(1)}, s32[512,1]{0,1:T(1,128)}, u32[]{:S(2)}) copy-start(s32[512,1]{0,1:T(1,128)} %param.19) | copy-start | bytes 6148
  10.5 7.7 %copy-start.8 = (s32[7]{0:T(128)S(1)}, s32[7]{0:T(128)}, u32[]{:S(2)}) copy-start(s32[7]{0:T(128)} %constant.130.clone) | copy-start | bytes 88
  10.5 7.7 %copy-start.9 = (s32[7]{0:T(128)S(1)}, s32[7]{0:T(128)}, u32[]{:S(2)}) copy-start(s32[7]{0:T(128)} %constant.129.clone) | copy-start | bytes 88
  10.5 8.1 %copy-start.7 = (s32[512]{0:T(512)S(1)}, s32[512]{0:T(512)}, u32[]{:S(2)}) copy-start(s32[512]{0:T(512)} %constant.135) | copy-start | bytes 6148
  12.6 9.2 %copy-start.10 = (s32[4,1,1]{0,2,1:T(1,128)S(1)}, s32[4,1,1]{0,2,1:T(1,128)}, u32[]{:S(2)}) copy-start(s32[4,1,1]{0,2,1:T(1,128)} %constant.133.clone) | copy-start | bytes 52
  12.6 16.7 %collective-permute-start = (bf16[2,96,384]{2,1,0:T(8,128)(2,1)}, bf16[2,96,384]{2,1,0:T(8,128)(2,1)S(1)}, u32[]{:S(2)}, u32[]{:S(2)}) collective-permute-start(bf16[2,96,384]{2,1,0:T(8,128)(2,1)} %get-tuple-element.8), channel_id=1, source_target_pairs={{0,4},{4,8},{8,12},{12,16},{16,20},{20,24},{24,28},{1,5},{5,9},{9,... | collective-permute-start | bytes 442376 | tf_op jit(solution)/shard_map/ppermute | solution.py:621
  14.0 15.3 %collective-permute-start.1 = (bf16[2,112,384]{2,1,0:T(8,128)(2,1)}, bf16[2,112,384]{2,1,0:T(8,128)(2,1)S(1)}, u32[]{:S(2)}, u32[]{:S(2)}) collective-permute-start(bf16[2,112,384]{2,1,0:T(8,128)(2,1)} %get-tuple-element.9), channel_id=1, source_target_pairs={{4,0},{8,4},{12,8},{16,12},{20,16},{24,20},{28,24},{5,1},{9,5},{13... | collective-permute-start | bytes 516104 | tf_op jit(solution)/shard_map/ppermute | solution.py:622
  18.5 10.4 %copy-start.4 = (s32[7]{0:T(128)}, s32[7]{0:T(128)S(1)}, u32[]{:S(2)}) copy-start(s32[7]{0:T(128)S(1)} %convert_reduce_fusion.1.count_ref) | copy-start | bytes 88
  22.8 6.1 %copy-start.6 = (s32[4,128]{1,0:T(4,128)S(1)}, s32[4,128]{1,0:T(4,128)}, u32[]{:S(2)}) copy-start(s32[4,128]{1,0:T(4,128)} %constant.134) | copy-start | bytes 6148
  29.3 0.7 copy-start.2
  29.3 0.7 copy-start.1
  44.7 9.9 %all-to-all-start = ((bf16[8,32,256]{2,1,0:T(8,128)(2,1)}), bf16[8,32,256]{2,1,0:T(8,128)(2,1)S(1)}, u32[]{:S(2)}, u32[]{:S(2)}) async-start(bf16[8,32,256]{2,1,0:T(8,128)(2,1)} %get-tuple-element.13), calls=%async_computation | async-start | bytes 262144 | tf_op jit(solution)/shard_map/all_to_all | solution.py:678
  63.6 30.0 %copy-start.5 = (s32[7]{0:T(128)S(1)}, s32[7]{0:T(128)}, u32[]{:S(2)}) copy-start(s32[7]{0:T(128)} %copy-done.4) | copy-start | bytes 88
  86.2 13.2 %all-to-all-start.1 = ((bf16[8,64,256]{2,1,0:T(8,128)(2,1)}), bf16[8,64,256]{2,1,0:T(8,128)(2,1)S(1)}, u32[]{:S(2)}, u32[]{:S(2)}) async-start(bf16[8,64,256]{2,1,0:T(8,128)(2,1)} %broadcast_in_dim.80), calls=%async_computation.1 | async-start | bytes 524288 | tf_op jit(solution)/shard_map/all_to_all | solution.py:607
